TPU v7x, 32 devices: a whole 2x2x4 slice. The times are simulated.
32 devices in a mesh: harm: 4 (over y, x), slab: 8 (over z, core).
Axes of the slice: x: 2, y: 2, z: 4, core: 2. Of those that a mesh axis runs over, the one named last changes fastest.
Arguments:
- krylov_basis: float32 [3, 4, 4, 16, 32, 128], P(None, 'harm', None, 'slab'), may hold values from -16 to 16
- weights: float32 [3], replicated, may hold values from -3 to 3
- base_flow: bfloat16 [4, 3, 16, 32, 128], P('harm', None, 'slab'), may hold values from -4 to 4
- shifts: float32 [4], P('harm'), may hold values from 0.25 to 2
Outputs:
- next_vector: float32 [4, 4, 16, 32, 128], P('harm', None, 'slab')
- arnoldi_column: float32 [4], replicated
All inputs are finite; a program needn't handle non-finite values.
Results may differ from a plain program's by a relative error of at most 0.009.
Values may be sent and summed in bfloat16 or wider, within the bound.
No kernel may reach another device: no remote copies, remote signals or barrier semaphores. Data moves between devices by JAX's collectives and lax.ppermute only.
A program may use at most 64 MiB of HBM per device.

v0:
```python
import jax
import jax.numpy as jnp
from jax import lax
from jax.sharding import PartitionSpec as P

SWEEPS = 4


viscosity = 1.0
epsilon = 1e-06


def padded_2(cells, sides, width):
    for axis, dim in sides:
        count = lax.axis_size(axis)
        ends = count - 1
        head = lax.slice_in_dim(cells, 0, width, axis=dim)
        tail = lax.slice_in_dim(cells, cells.shape[dim] - width, cells.shape[dim], axis=dim)
        cells = jnp.concatenate(
            [
                lax.ppermute(tail, axis, [(i, (i + 1) % count) for i in range(ends)]),
                cells,
                lax.ppermute(head, axis, [((i + 1) % count, i) for i in range(ends)]),
            ],
            axis=dim,
        )
    return cells


def broadcast(x, axis, root):
    mine = lax.axis_index(axis) == root
    return lax.psum(jnp.where(mine, x, jnp.zeros_like(x)), axis)


def shifted(value, axis, steps):
    count = lax.axis_size(axis)
    pairs = [(source, (source + steps) % count) for source in range(count)]
    return lax.ppermute(value, axis, pairs)


def neighbours_y(values):
    padded = jnp.pad(values, ((0, 0), (0, 0), (1, 1), (0, 0)))
    return (padded[:, :, 2:], padded[:, :, :-2])


def laplace_ext(extended):
    center = extended[:, 1:-1]
    upper_y, lower_y = neighbours_y(center)
    result = extended[:, 2:] + extended[:, :-2] + upper_y + lower_y
    result = result + jnp.roll(center, -1, axis=3) + jnp.roll(center, 1, axis=3)
    return result - 6.0 * center


def divergence_split(flux_x, flux_y, flux_z):
    upper_y, lower_y = neighbours_y(flux_y)
    result = 0.5 * (flux_x[:, 2:] - flux_x[:, :-2])
    result = result + 0.5 * (upper_y - lower_y)
    return result + 0.5 * (jnp.roll(flux_z, -1, axis=3) - jnp.roll(flux_z, 1, axis=3))


def sweep_extend(values):
    return padded_2(values, (("slab", 1),), 1)


def chebyshev(applied, shift_value):
    middle = shift_value + 6.0 * viscosity
    half_span = 6.0 * viscosity
    span_ratio = middle / half_span
    solution = jnp.zeros_like(applied)
    remainder = applied
    direction = applied / middle
    ratio_prev = 1.0 / span_ratio
    for sweep_index in range(SWEEPS):
        solution = solution + direction
        remainder = remainder - (
            shift_value * direction - viscosity * laplace_ext(sweep_extend(direction))
        )
        ratio_next = 1.0 / (2.0 * span_ratio - ratio_prev)
        direction = ratio_next * ratio_prev * direction + 2.0 * ratio_next / half_span * remainder
        ratio_prev = ratio_next
    return solution + direction


def shards(krylov_basis, weights, base_flow, shifts):
    vectors = krylov_basis[:, 0]
    start_vec = jnp.sum(weights[:, None, None, None, None] * vectors, axis=0)
    harm_count = lax.axis_size("harm") * base_flow.shape[0]
    local_flow = base_flow[0]
    cell_shape = start_vec.shape
    empty = jnp.zeros((3,) + cell_shape, jnp.float32)

    def add_term(fluxes, current, cycle_step):
        shared = broadcast(local_flow, "harm", cycle_step).astype(jnp.float32)
        return fluxes + shared[:, None] * current[None]

    def advance(cycle_step, carried):
        fluxes, current = carried
        fluxes = add_term(fluxes, current, cycle_step)
        return (fluxes, shifted(current, "harm", 1))

    fluxes, current = lax.fori_loop(0, harm_count - 1, advance, (empty, start_vec))
    fluxes = add_term(fluxes, current, harm_count - 1)
    fluxes = fluxes.reshape((12,) + cell_shape[1:])
    stacked = jnp.concatenate([fluxes, start_vec], axis=0)
    extended = padded_2(stacked, (("slab", 1),), 1)
    moved = divergence_split(extended[0:4], extended[4:8, 1:-1], extended[8:12, 1:-1])
    field_ext = extended[12:]
    own_shift = shifts[0]
    applied = own_shift * start_vec - viscosity * laplace_ext(field_ext) + moved
    solution = chebyshev(applied, own_shift)
    entries = float(
        harm_count
        * cell_shape[0]
        * cell_shape[1]
        * lax.axis_size("slab")
        * cell_shape[2]
        * cell_shape[3]
    )
    local_proj = jnp.sum(vectors * solution[None], axis=(1, 2, 3, 4))
    projection = lax.psum(local_proj, ("harm", "slab")) / entries
    residue = solution - jnp.sum(projection[:, None, None, None, None] * vectors, axis=0)
    square = lax.psum(jnp.sum(residue * residue), ("harm", "slab")) / entries
    norm_value = jnp.sqrt(square + epsilon)
    next_vector = (residue / norm_value)[None]
    arnoldi_column = jnp.concatenate([projection, norm_value[None]])
    return (next_vector, arnoldi_column)


def solution(mesh):
    in_specs = (
        P(None, "harm", None, "slab", None, None),
        P(),
        P("harm", None, "slab", None, None),
        P("harm"),
    )
    out_specs = (P("harm", None, "slab", None, None), P())
    return jax.shard_map(shards, mesh=mesh, in_specs=in_specs, out_specs=out_specs, check_vma=False)
```

profile of v0, /device:TPU:0, one launch (start us, length us, event | category | flops | bytes accessed | tf_op | source)
XLA Modules:
  0.0 199.5 jit_solution(12436300417976476142)
XLA Ops:
  0.7 0.6 copy-done.5
  1.3 1.1 fusion
  2.4 0.6 copy-done
  3.1 0.2 copy-done.4
  3.3 18.4 %psum.32 = bf16[3,2,32,128]{3,2,1,0:T(8,128)(2,1)S(1)} all-reduce(bf16[3,2,32,128]{3,2,1,0:T(8,128)(2,1)S(1)} %broadcast_select_fusion.1), channel_id=1, replica_groups=mesh['harm'=4,'slab'=8] {'harm'}, use_global_device_ids=true, to_apply=%region_4.5 | all-reduce | flops 24576 | bytes 98304 | tf_op jit(solution)/shard_map/psum | solution.py:32
  21.7 52.6 %while.16 = (s32[]{:T(128)}, f32[3,4,2,32,128]{4,3,2,1,0:T(8,128)S(1)}, f32[4,2,32,128]{3,2,1,0:T(8,128)S(1)}, bf16[3,2,32,128]{3,2,1,0:T(8,128)(2,1)S(1)}, s32[]{:T(128)}, /*index=5*/u32[]{:T(128)}, s32[]{:T(128)}) while((s32[]{:T(128)}, f32[3,4,2,32,128]{4,3,2,1,0:T(8,128)S(1)}, f32[4,2,32,128]{3,2,1,0:T(8,128)S(1)}, ...), condition=%wide.region_3.4_spmd.clone, body=%wide.region_1.3_spmd.clone.sunk | while | flops 368647 | bytes 2146473 | solution.py:101
  21.8 17.2 %psum.37 = bf16[3,2,32,128]{3,2,1,0:T(8,128)(2,1)S(1)} all-reduce(bf16[3,2,32,128]{3,2,1,0:T(8,128)(2,1)S(1)} %broadcast_select_fusion.3), channel_id=1, replica_groups=mesh['harm'=4,'slab'=8] {'harm'}, use_global_device_ids=true, to_apply=%region_2.2 | all-reduce | flops 24576 | bytes 98304 | tf_op jit(solution)/shard_map/while/body/eval_jaxpr/psum | solution.py:32
  39.4 17.3 %psum.37 = bf16[3,2,32,128]{3,2,1,0:T(8,128)(2,1)S(1)} all-reduce(bf16[3,2,32,128]{3,2,1,0:T(8,128)(2,1)S(1)} %broadcast_select_fusion.3), channel_id=1, replica_groups=mesh['harm'=4,'slab'=8] {'harm'}, use_global_device_ids=true, to_apply=%region_2.2 | all-reduce | flops 24576 | bytes 98304 | tf_op jit(solution)/shard_map/while/body/eval_jaxpr/psum | solution.py:32
  56.9 17.1 %psum.37 = bf16[3,2,32,128]{3,2,1,0:T(8,128)(2,1)S(1)} all-reduce(bf16[3,2,32,128]{3,2,1,0:T(8,128)(2,1)S(1)} %broadcast_select_fusion.3), channel_id=1, replica_groups=mesh['harm'=4,'slab'=8] {'harm'}, use_global_device_ids=true, to_apply=%region_2.2 | all-reduce | flops 24576 | bytes 98304 | tf_op jit(solution)/shard_map/while/body/eval_jaxpr/psum | solution.py:32
  74.3 0.8 copy-done.1
  75.2 1.3 collective-permute-start.1
  76.5 3.0 %collective-permute-start.2 = (f32[16,1,32,128]{3,2,1,0:T(8,128)S(1)}, f32[16,1,32,128]{3,2,1,0:T(8,128)S(1)}, u32[]{:S(2)}, u32[]{:S(2)}) collective-permute-start(f32[16,1,32,128]{3,2,1,0:T(8,128)S(1)} %get-tuple-element.118), channel_id=1, source_target_pairs={{0,1},{1,2},{2,3},{3,4},{4,5},{5,6},{6,7},{8,9},{9,10},{10,11},{11... | collective-permute-start | bytes 786440 | tf_op jit(solution)/shard_map/ppermute | solution.py:21
  80.9 0.2 broadcast_divide_fusion
  81.2 1.3 collective-permute-start.3
  82.5 5.7 %collective-permute-start.4 = (f32[4,1,32,128]{3,2,1,0:T(8,128)S(1)}, f32[4,1,32,128]{3,2,1,0:T(8,128)S(1)}, u32[]{:S(2)}, u32[]{:S(2)}) collective-permute-start(f32[4,1,32,128]{3,2,1,0:T(8,128)S(1)} %get-tuple-element.140), channel_id=1, source_target_pairs={{0,1},{1,2},{2,3},{3,4},{4,5},{5,6},{6,7},{8,9},{9,10},{10,11},{11... | collective-permute-start | bytes 196616 | tf_op jit(solution)/shard_map/ppermute | solution.py:21
  88.3 0.8 collective-permute-done.4
  89.4 1.3 collective-permute-start.5
  90.7 5.4 %collective-permute-start.6 = (f32[4,1,32,128]{3,2,1,0:T(8,128)S(1)}, f32[4,1,32,128]{3,2,1,0:T(8,128)S(1)}, u32[]{:S(2)}, u32[]{:S(2)}) collective-permute-start(f32[4,1,32,128]{3,2,1,0:T(8,128)S(1)} %get-tuple-element.134), channel_id=1, source_target_pairs={{0,1},{1,2},{2,3},{3,4},{4,5},{5,6},{6,7},{8,9},{9,10},{10,11},{11... | collective-permute-start | bytes 196616 | tf_op jit(solution)/shard_map/ppermute | solution.py:21
  96.2 0.8 collective-permute-done.6
  97.3 1.3 collective-permute-start.7
  98.6 5.3 %collective-permute-start.8 = (f32[4,1,32,128]{3,2,1,0:T(8,128)S(1)}, f32[4,1,32,128]{3,2,1,0:T(8,128)S(1)}, u32[]{:S(2)}, u32[]{:S(2)}) collective-permute-start(f32[4,1,32,128]{3,2,1,0:T(8,128)S(1)} %get-tuple-element.128), channel_id=1, source_target_pairs={{0,1},{1,2},{2,3},{3,4},{4,5},{5,6},{6,7},{8,9},{9,10},{10,11},{11... | collective-permute-start | bytes 196616 | tf_op jit(solution)/shard_map/ppermute | solution.py:21
  104.0 0.8 collective-permute-done.8
  105.1 4.7 %collective-permute-start.10 = (f32[4,1,32,128]{3,2,1,0:T(8,128)S(1)}, f32[4,1,32,128]{3,2,1,0:T(8,128)S(1)}, u32[]{:S(2)}, u32[]{:S(2)}) collective-permute-start(f32[4,1,32,128]{3,2,1,0:T(8,128)S(1)} %get-tuple-element.126), channel_id=1, source_target_pairs={{0,1},{1,2},{2,3},{3,4},{4,5},{5,6},{6,7},{8,9},{9,10},{10,11},{11... | collective-permute-start | bytes 196616 | tf_op jit(solution)/shard_map/ppermute | solution.py:21
  109.8 1.3 collective-permute-start.9
  111.2 3.6 %collective-permute-done.9 = f32[4,1,32,128]{3,2,1,0:T(8,128)S(1)} collective-permute-done((f32[4,1,32,128]{3,2,1,0:T(8,128)S(1)}, f32[4,1,32,128]{3,2,1,0:T(8,128)S(1)}, u32[]{:S(2)}, u32[]{:S(2)}) %collective-permute-start.9) | collective-permute-done | bytes 65568 | tf_op jit(solution)/shard_map/ppermute | solution.py:23
  114.8 0.2 fusion.45
  114.9 0.8 copy-done.3
  115.9 40.9 %psum.33 = f32[3]{0:T(128)S(1)} all-reduce(f32[3]{0:T(128)S(1)} %fusion.1), channel_id=1, replica_groups=mesh['harm'=4,'slab'=8] {'harm','slab'}, use_global_device_ids=true, to_apply=%region_6.7 | all-reduce | flops 3 | bytes 24 | tf_op jit(solution)/shard_map/psum | solution.py:120
  157.0 0.6 multiply_reduce_fusion
  157.6 39.9 %psum.34 = f32[]{:T(128)} all-reduce(f32[]{:T(128)} %get-tuple-element.107), channel_id=1, replica_groups=mesh['harm'=4,'slab'=8] {'harm','slab'}, use_global_device_ids=true, to_apply=%region_9.10 | all-reduce | flops 1 | bytes 8 | tf_op jit(solution)/shard_map/psum | solution.py:122
  198.2 0.6 pad_maximum_fusion.13
  198.8 0.7 divide_bitcast_fusion
  (59 shorter events, 2.7 us)
Async XLA Ops:
  0.6 0.7 copy-start.5
  2.4 0.7 copy-start
  2.4 0.8 copy-start.4
  3.3 18.4 %copy-start.2 = (f32[4,2,32,128]{3,2,1,0:T(8,128)S(1)}, f32[4,2,32,128]{3,2,1,0:T(8,128)}, u32[]{:S(2)}) copy-start(f32[4,2,32,128]{3,2,1,0:T(8,128)} %copy-done) | copy-start | bytes 393220
  21.7 17.5 %collective-permute-start = (f32[4,2,32,128]{3,2,1,0:T(8,128)S(1)}, f32[4,2,32,128]{3,2,1,0:T(8,128)S(1)}, u32[]{:S(2)}, u32[]{:S(2)}) collective-permute-start(f32[4,2,32,128]{3,2,1,0:T(8,128)S(1)} %copy.11), channel_id=1, source_target_pairs={{0,8},{8,16},{16,24},{24,0},{1,9},{9,17},{17,25},{25,1},{2,10},{10... | collective-permute-start | bytes 393224 | tf_op jit(solution)/shard_map/while/body/eval_jaxpr/ppermute | solution.py:38
  39.3 17.5 %collective-permute-start = (f32[4,2,32,128]{3,2,1,0:T(8,128)S(1)}, f32[4,2,32,128]{3,2,1,0:T(8,128)S(1)}, u32[]{:S(2)}, u32[]{:S(2)}) collective-permute-start(f32[4,2,32,128]{3,2,1,0:T(8,128)S(1)} %copy.11), channel_id=1, source_target_pairs={{0,8},{8,16},{16,24},{24,0},{1,9},{9,17},{17,25},{25,1},{2,10},{10... | collective-permute-start | bytes 393224 | tf_op jit(solution)/shard_map/while/body/eval_jaxpr/ppermute | solution.py:38
  56.8 17.4 %collective-permute-start = (f32[4,2,32,128]{3,2,1,0:T(8,128)S(1)}, f32[4,2,32,128]{3,2,1,0:T(8,128)S(1)}, u32[]{:S(2)}, u32[]{:S(2)}) collective-permute-start(f32[4,2,32,128]{3,2,1,0:T(8,128)S(1)} %copy.11), channel_id=1, source_target_pairs={{0,8},{8,16},{16,24},{24,0},{1,9},{9,17},{17,25},{25,1},{2,10},{10... | collective-permute-start | bytes 393224 | tf_op jit(solution)/shard_map/while/body/eval_jaxpr/ppermute | solution.py:38
  74.3 0.9 copy-start.1
  75.2 5.7 %collective-permute-start.1 = (f32[16,1,32,128]{3,2,1,0:T(8,128)S(1)}, f32[16,1,32,128]{3,2,1,0:T(8,128)S(1)}, u32[]{:S(2)}, u32[]{:S(2)}) collective-permute-start(f32[16,1,32,128]{3,2,1,0:T(8,128)S(1)} %get-tuple-element.117), channel_id=1, source_target_pairs={{1,0},{2,1},{3,2},{4,3},{5,4},{6,5},{7,6},{9,8},{10,9},{11,10},{12... | collective-permute-start | bytes 786440 | tf_op jit(solution)/shard_map/ppermute | solution.py:23
  76.5 4.4 %collective-permute-start.2 = (f32[16,1,32,128]{3,2,1,0:T(8,128)S(1)}, f32[16,1,32,128]{3,2,1,0:T(8,128)S(1)}, u32[]{:S(2)}, u32[]{:S(2)}) collective-permute-start(f32[16,1,32,128]{3,2,1,0:T(8,128)S(1)} %get-tuple-element.118), channel_id=1, source_target_pairs={{0,1},{1,2},{2,3},{3,4},{4,5},{5,6},{6,7},{8,9},{9,10},{10,11},{11... | collective-permute-start | bytes 786440 | tf_op jit(solution)/shard_map/ppermute | solution.py:21
  81.2 7.1 %collective-permute-start.3 = (f32[4,1,32,128]{3,2,1,0:T(8,128)S(1)}, f32[4,1,32,128]{3,2,1,0:T(8,128)S(1)}, u32[]{:S(2)}, u32[]{:S(2)}) collective-permute-start(f32[4,1,32,128]{3,2,1,0:T(8,128)S(1)} %get-tuple-element.139), channel_id=1, source_target_pairs={{1,0},{2,1},{3,2},{4,3},{5,4},{6,5},{7,6},{9,8},{10,9},{11,10},{12... | collective-permute-start | bytes 196616 | tf_op jit(solution)/shard_map/ppermute | solution.py:23
  82.5 6.6 %collective-permute-start.4 = (f32[4,1,32,128]{3,2,1,0:T(8,128)S(1)}, f32[4,1,32,128]{3,2,1,0:T(8,128)S(1)}, u32[]{:S(2)}, u32[]{:S(2)}) collective-permute-start(f32[4,1,32,128]{3,2,1,0:T(8,128)S(1)} %get-tuple-element.140), channel_id=1, source_target_pairs={{0,1},{1,2},{2,3},{3,4},{4,5},{5,6},{6,7},{8,9},{9,10},{10,11},{11... | collective-permute-start | bytes 196616 | tf_op jit(solution)/shard_map/ppermute | solution.py:21
  89.4 6.9 %collective-permute-start.5 = (f32[4,1,32,128]{3,2,1,0:T(8,128)S(1)}, f32[4,1,32,128]{3,2,1,0:T(8,128)S(1)}, u32[]{:S(2)}, u32[]{:S(2)}) collective-permute-start(f32[4,1,32,128]{3,2,1,0:T(8,128)S(1)} %get-tuple-element.133), channel_id=1, source_target_pairs={{1,0},{2,1},{3,2},{4,3},{5,4},{6,5},{7,6},{9,8},{10,9},{11,10},{12... | collective-permute-start | bytes 196616 | tf_op jit(solution)/shard_map/ppermute | solution.py:23
  90.7 6.3 %collective-permute-start.6 = (f32[4,1,32,128]{3,2,1,0:T(8,128)S(1)}, f32[4,1,32,128]{3,2,1,0:T(8,128)S(1)}, u32[]{:S(2)}, u32[]{:S(2)}) collective-permute-start(f32[4,1,32,128]{3,2,1,0:T(8,128)S(1)} %get-tuple-element.134), channel_id=1, source_target_pairs={{0,1},{1,2},{2,3},{3,4},{4,5},{5,6},{6,7},{8,9},{9,10},{10,11},{11... | collective-permute-start | bytes 196616 | tf_op jit(solution)/shard_map/ppermute | solution.py:21
  97.3 6.7 %collective-permute-start.7 = (f32[4,1,32,128]{3,2,1,0:T(8,128)S(1)}, f32[4,1,32,128]{3,2,1,0:T(8,128)S(1)}, u32[]{:S(2)}, u32[]{:S(2)}) collective-permute-start(f32[4,1,32,128]{3,2,1,0:T(8,128)S(1)} %get-tuple-element.127), channel_id=1, source_target_pairs={{1,0},{2,1},{3,2},{4,3},{5,4},{6,5},{7,6},{9,8},{10,9},{11,10},{12... | collective-permute-start | bytes 196616 | tf_op jit(solution)/shard_map/ppermute | solution.py:23
  98.6 6.2 %collective-permute-start.8 = (f32[4,1,32,128]{3,2,1,0:T(8,128)S(1)}, f32[4,1,32,128]{3,2,1,0:T(8,128)S(1)}, u32[]{:S(2)}, u32[]{:S(2)}) collective-permute-start(f32[4,1,32,128]{3,2,1,0:T(8,128)S(1)} %get-tuple-element.128), channel_id=1, source_target_pairs={{0,1},{1,2},{2,3},{3,4},{4,5},{5,6},{6,7},{8,9},{9,10},{10,11},{11... | collective-permute-start | bytes 196616 | tf_op jit(solution)/shard_map/ppermute | solution.py:21
  105.1 6.1 %collective-permute-start.10 = (f32[4,1,32,128]{3,2,1,0:T(8,128)S(1)}, f32[4,1,32,128]{3,2,1,0:T(8,128)S(1)}, u32[]{:S(2)}, u32[]{:S(2)}) collective-permute-start(f32[4,1,32,128]{3,2,1,0:T(8,128)S(1)} %get-tuple-element.126), channel_id=1, source_target_pairs={{0,1},{1,2},{2,3},{3,4},{4,5},{5,6},{6,7},{8,9},{9,10},{10,11},{11... | collective-permute-start | bytes 196616 | tf_op jit(solution)/shard_map/ppermute | solution.py:21
  109.8 5.0 %collective-permute-start.9 = (f32[4,1,32,128]{3,2,1,0:T(8,128)S(1)}, f32[4,1,32,128]{3,2,1,0:T(8,128)S(1)}, u32[]{:S(2)}, u32[]{:S(2)}) collective-permute-start(f32[4,1,32,128]{3,2,1,0:T(8,128)S(1)} %get-tuple-element.125), channel_id=1, source_target_pairs={{1,0},{2,1},{3,2},{4,3},{5,4},{6,5},{7,6},{9,8},{10,9},{11,10},{12... | collective-permute-start | bytes 196616 | tf_op jit(solution)/shard_map/ppermute | solution.py:23
  114.8 1.0 copy-start.3
where the time goes:
time: 200 us; the launch traced here: 199 us
  blocking collectives  151 us (76%)
  starting transfers between devices  30.8 us (15%)
  waiting for transfers between devices  5.94 us (3%)
  other arithmetic  4.62 us (2%)
  local copies, waits for them, and re-layouts  4.36 us (2%)
  between operations  2.59 us (1%)
    psum x4, blocking collectives, broadcast(): return lax.psum(jnp.where(mine, x, jnp.zeros_like(x)), axis)  70 us
    psum x1, blocking collectives, shards(): projection = lax.psum(local_proj, ('harm', 'slab')) / entries  40.9 us
    psum x1, blocking collectives, shards(): square = lax.psum(jnp.sum(residue * residue), ('harm', 'slab')) / entries  39.9 us
    ppermute x5, starting transfers between devices, padded_2(): lax.ppermute(tail, axis, [(i, (i + 1) % count) for i in range(ends)])  24.2 us
    ppermute x5, starting transfers between devices, padded_2(): lax.ppermute(head, axis, [((i + 1) % count, i) for i in range(ends)])  6.46 us
  transfers between devices with their start and end apart: 13, of which 4 were waited for; matrix products, arithmetic and copies ran while one was open for 1% of the time, Pallas kernels for 0%

commit v1 on v0

v1 whole, which is shorter than its diff:
```python
import math

import jax
import jax.numpy as jnp
from jax import lax
from jax.experimental import pallas as pl
from jax.experimental.pallas import tpu as pltpu
from jax.sharding import PartitionSpec as P

SWEEPS = 4
DIRS = 3
VISCOSITY = 1.0
EPSILON = 1e-06
BASIS_MAX, WEIGHT_MAX, FLOW_MAX, SHIFT_MAX = 16.0, 3.0, 4.0, 2.0
SENT_MAX = 60000.0
F32 = jnp.float32
SENT = jnp.float16
VMEM = pl.BlockSpec(memory_space=pltpu.VMEM)
SMEM = pl.BlockSpec(memory_space=pltpu.SMEM)


def call(body, out_shape, args, specs, out_specs, scratch=()):
    return pl.pallas_call(
        body, out_shape=out_shape, in_specs=specs, out_specs=out_specs, scratch_shapes=scratch,
        compiler_params=pltpu.CompilerParams(vmem_limit_bytes=8 << 20),
    )(*args)


def rows(shape):
    return lax.broadcasted_iota(jnp.int32, shape, len(shape) - 2)


def y_up(plane):
    count = plane.shape[-2]
    return jnp.where(rows(plane.shape) < count - 1, pltpu.roll(plane, count - 1, plane.ndim - 2), 0.0)


def y_down(plane):
    return jnp.where(rows(plane.shape) > 0, pltpu.roll(plane, 1, plane.ndim - 2), 0.0)


def z_up(plane):
    return pltpu.roll(plane, plane.shape[-1] - 1, plane.ndim - 1)


def z_down(plane):
    return pltpu.roll(plane, 1, plane.ndim - 1)


def parity():
    return lax.rem(lax.axis_index("slab"), 2)


def scales(count, harmonics):
    vector = count * WEIGHT_MAX * BASIS_MAX
    flux = harmonics * FLOW_MAX * vector
    applied = (SHIFT_MAX + 12.0 * VISCOSITY) * vector + DIRS * flux
    return [2.0 ** math.floor(math.log2(SENT_MAX / bound)) for bound in (vector, applied)]


def start_kernel(basis_in, weights_in, flow_in, basis, vec, message, weights, flow, sems, *, rescale):
    count, fields = basis.shape[0], basis.shape[2]
    copies = [pltpu.make_async_copy(weights_in, weights, sems.at[0])]
    copies.append(pltpu.make_async_copy(flow_in, flow, sems.at[1]))
    copies += [pltpu.make_async_copy(basis_in.at[j], basis.at[j], sems.at[2 + j]) for j in range(count)]
    for copy in copies:
        copy.start()
    for copy in copies:
        copy.wait()
    for f in range(fields):
        total = weights[0] * basis[0, 0, f]
        for j in range(1, count):
            total = total + weights[j] * basis[j, 0, f]
        vec[f] = total
        message[f] = total * rescale
    message[fields:] = flow[0].astype(F32)


def gram_kernel(basis, sums):
    count = basis.shape[0]
    lanes = lax.broadcasted_iota(jnp.int32, sums.shape, 1)
    line, place = jnp.zeros(sums.shape, F32), 1 + count
    for i in range(count):
        for j in range(i, count):
            line = jnp.where(lanes == place, jnp.sum(basis[i, 0] * basis[j, 0]), line)
            place += 1
    sums[...] = line


def flux_kernel(shift, vec, *refs, harmonics, unscale, rescale):
    messages = refs[:harmonics]
    partial, away, away_sent, flows = refs[harmonics:]
    fields, planes = vec.shape[0], vec.shape[1]
    harm = lax.axis_index("harm")
    core = parity()
    sign = 0.5 * (1 - 2 * core).astype(F32)
    flip = core == 1
    for j in range(harmonics):
        flow = messages[0][...].astype(F32) if j == 0 else messages[j][fields:]
        flows[lax.rem(harm - j + harmonics, harmonics)] = flow
    own = shift[0] + 6.0 * VISCOSITY
    for f in range(fields):
        local, plus, minus = [], [], []
        for t in range(planes):
            x = jnp.where(flip, planes - 1 - t, t)
            center = vec[f, x]
            flux = [flows[0, d, x] * center for d in range(DIRS)]
            for j in range(1, harmonics):
                other = messages[j][f, x] * unscale
                flux = [flux[d] + flows[j, d, x] * other for d in range(DIRS)]
            half_y = 0.5 * flux[1]
            half_z = 0.5 * flux[2]
            half_x = sign * flux[0]
            value = own * center + y_up(half_y - VISCOSITY * center) - y_down(half_y + VISCOSITY * center)
            value = value + z_up(half_z - VISCOSITY * center) - z_down(half_z + VISCOSITY * center)
            local.append(value)
            plus.append(half_x - VISCOSITY * center)
            minus.append(-half_x - VISCOSITY * center)
        for t in range(planes):
            value = local[t]
            if t + 1 < planes:
                value = value + plus[t + 1]
            if t > 0:
                value = value + minus[t - 1]
            partial[t, f] = value
        partial[planes, f] = minus[planes - 1]
        away[f] = plus[0]
        away_sent[f] = plus[0] * rescale


def chip_kernel(mine, theirs, away, message, *, rescale):
    planes = mine.shape[0] - 1
    for t in range(planes):
        own, other = mine[t], theirs[planes - 1 - t]
        if t == planes - 1:
            own = own + theirs[planes]
        if t == 0:
            other = other + mine[planes]
        message[t] = own * rescale
        message[planes + t] = other * rescale
    message[2 * planes] = away[...] * rescale


def inner_kernel(mine, theirs, away, outer, message, *, unscale):
    planes = mine.shape[0] - 1
    message[0] = outer[0] * unscale + away[...]
    for t in range(1, planes):
        message[t] = outer[t] * unscale
    own = mine[0] + outer[2 * planes] * unscale
    if planes == 1:
        own = own + theirs[planes]
    message[planes] = own


def chebyshev_kernel(shift, gram, basis, vec, mine, theirs, away, outer, inner, far, change, sums, *, unscale):
    count, fields = basis.shape[0], vec.shape[0]
    planes = mine.shape[0] - 1
    slab, slabs = lax.axis_index("slab"), lax.axis_size("slab")
    core = parity()
    flip = core == 1
    chip, chips = lax.div(slab, 2), slabs // 2
    has_low = (chip > 0).astype(F32)
    has_high = (chip < chips - 1).astype(F32)
    has_outer = jnp.where(flip, has_high, has_low)
    has_inner = jnp.where(flip, has_low, has_high)
    two_away = jnp.where(flip, chips - 1 - chip, chip) > 1
    has_far = two_away.astype(F32)
    own_shift = shift[0]
    middle = own_shift + 6.0 * VISCOSITY
    half_span = 6.0 * VISCOSITY
    span_ratio = middle / half_span
    ratio = 1.0 / span_ratio
    gains, far_gain = [], 1.0 / middle
    for _ in range(SWEEPS):
        following = 1.0 / (2.0 * span_ratio - ratio)
        gains.append((following * ratio, 2.0 * following / half_span))
        far_gain = far_gain * (gains[-1][1] * VISCOSITY)
        ratio = following
    depth = SWEEPS
    first = 1.0 / middle
    totals = [None] * (1 + count)
    for f in range(fields):
        remainder = [outer[depth - 1 - i, f] * unscale for i in range(depth - 1)]
        remainder.append(outer[0, f] * unscale + away[f])
        scale = [has_outer] * depth + [None] * (2 * planes) + [has_inner] * planes
        for t in range(planes):
            value = mine[t, f]
            if t == planes - 1:
                value = value + theirs[planes, f]
            if t == 0:
                value = value + outer[2 * planes, f] * unscale
            remainder.append(value)
        for t in range(planes - 1, -1, -1):
            if t == 0:
                remainder.append(inner[planes, f])
            elif t == planes - 1:
                remainder.append(theirs[t, f] + mine[planes, f])
            else:
                remainder.append(theirs[t, f])
        for t in range(planes):
            remainder.append(inner[t, f])
        direction = [
            (r * first) if m is None else (r * (first * m)) for r, m in zip(remainder, scale)
        ]
        solution = [direction[depth + t] for t in range(planes)]
        low = 0
        for sweep in range(SWEEPS):
            keep, gain = gains[sweep]
            nothing = low + 1
            end = low + len(direction) - 1
            next_remainder, next_direction = [], []
            for position in range(nothing, end):
                i = position - low
                d = direction[i]
                around = direction[i + 1] + direction[i - 1] + y_up(d) + y_down(d) + z_up(d) + z_down(d)
                r = remainder[i] - (middle * d - VISCOSITY * around)
                m = scale[position]
                if m is None:
                    n = keep * d + gain * r
                else:
                    n = (keep * m) * d + (gain * m) * r
                next_remainder.append(r)
                next_direction.append(n)
            remainder, direction, low = next_remainder, next_direction, low + 1
            solution = [s + direction[depth - low + t] for t, s in enumerate(solution)]
        solution[0] = solution[0] + (far_gain * unscale * has_far) * far[f]
        for t in range(planes):
            x = jnp.where(flip, planes - 1 - t, t)
            moved = solution[t] - vec[f, x]
            change[f, x] = moved
            parts = [moved * moved] + [basis[j, 0, f, x] * moved for j in range(count)]
            totals = [p if q is None else q + p for q, p in zip(totals, parts)]
    lanes = lax.broadcasted_iota(jnp.int32, (1, sums.shape[-1]), 1)
    line = gram[...]
    place = 0
    for total in totals:
        line = jnp.where(lanes == place, jnp.sum(total), line)
        place += 1
    sums[...] = jnp.broadcast_to(line[None], sums.shape)


def final_kernel(weights, basis, change, sums, vector, column, *, entries):
    count = basis.shape[0]
    line = jnp.sum(sums[:, 0, :], axis=0, keepdims=True) * (1.0 / entries)
    lanes = lax.broadcasted_iota(jnp.int32, line.shape, 1)

    def entry(place):
        return jnp.sum(jnp.where(lanes == place, line, 0.0))

    square = entry(0)
    moved = [entry(1 + j) for j in range(count)]
    gram, place = {}, 1 + count
    for i in range(count):
        for j in range(i, count):
            gram[i, j] = gram[j, i] = entry(place)
            place += 1
    projection, excess = [], []
    for j in range(count):
        value = moved[j]
        for i in range(count):
            value = value + weights[i] * gram[i, j]
        projection.append(value)
        excess.append(value - weights[j])
    for j in range(count):
        inner = -2.0 * moved[j]
        for i in range(count):
            inner = inner + excess[i] * gram[i, j]
        square = square + excess[j] * inner
    norm = jnp.sqrt(jnp.full((1, line.shape[-1]), jnp.maximum(square, 0.0) + EPSILON, F32))
    inverse = (1.0 / norm)[:, None, None, :]
    residue = change[...]
    for j in range(count):
        residue = residue - excess[j] * basis[j, 0]
    vector[0] = residue * inverse
    for j in range(count):
        column[j] = projection[j]
    column[count] = jnp.max(norm)


def shards(krylov_basis, weights, base_flow, shifts):
    count, _, fields, planes, ny, nz = krylov_basis.shape
    harmonics, slabs = lax.axis_size("harm"), lax.axis_size("slab")
    assert 2 * planes == SWEEPS and slabs % 2 == 0
    shape = (fields, planes, ny, nz)
    vec_scale, applied_scale = scales(count, harmonics)

    def start_body(*refs):
        start_kernel(*refs, rescale=vec_scale)

    basis, vec, message = call(
        start_body,
        [
            jax.ShapeDtypeStruct(krylov_basis.shape, F32),
            jax.ShapeDtypeStruct(shape, F32),
            jax.ShapeDtypeStruct((fields + DIRS, planes, ny, nz), F32),
        ],
        [pltpu.with_memory_space_constraint(x, pltpu.HBM) for x in (krylov_basis, weights, base_flow)],
        [pl.BlockSpec(memory_space=pltpu.HBM)] * 3,
        [VMEM] * 3,
        [
            pltpu.SMEM(weights.shape, F32),
            pltpu.VMEM(base_flow.shape, base_flow.dtype),
            pltpu.SemaphoreType.DMA((2 + count,)),
        ],
    )
    message = message.astype(SENT)
    gram = call(gram_kernel, jax.ShapeDtypeStruct((1, nz), F32), (basis,), [VMEM], VMEM)
    messages = [base_flow[0]] + [
        lax.ppermute(message, "harm", [(i, (i + j) % harmonics) for i in range(harmonics)]).astype(F32)
        for j in range(1, harmonics)
    ]

    def flux_body(*refs):
        flux_kernel(*refs, harmonics=harmonics, unscale=1.0 / vec_scale, rescale=applied_scale)

    mine, away, away_sent = call(
        flux_body,
        [
            jax.ShapeDtypeStruct((planes + 1, fields, ny, nz), F32),
            jax.ShapeDtypeStruct((fields, ny, nz), F32),
            jax.ShapeDtypeStruct((fields, ny, nz), F32),
        ],
        (shifts, vec, *messages),
        [SMEM] + [VMEM] * (1 + harmonics),
        [VMEM] * 3,
        [pltpu.VMEM((harmonics, DIRS, planes, ny, nz), F32)],
    )
    swap = [(i, i ^ 1) for i in range(slabs)]
    links = [(i, i + 1) for i in range(1, slabs - 1, 2)]
    cross = links + [(b, a) for a, b in links]
    skips = [(i, i + 3) for i in range(1, slabs - 3, 2)]
    beyond = skips + [(b, a) for a, b in skips]
    theirs = lax.ppermute(mine, "slab", swap)

    def chip_body(*refs):
        chip_kernel(*refs, rescale=applied_scale)

    chip = call(
        chip_body,
        jax.ShapeDtypeStruct((2 * planes + 1, fields, ny, nz), F32),
        (mine, theirs, away),
        [VMEM] * 3,
        VMEM,
    )
    outer = lax.ppermute(chip.astype(SENT), "slab", cross).astype(F32)
    masks = {a ^ b for a, b in beyond}
    if len(masks) == 1 and slabs & (slabs - 1) == 0:
        beyond = [(i, i ^ mask) for i in range(slabs) for mask in masks]
    far = lax.ppermute(away_sent.astype(SENT), "slab", beyond).astype(F32)

    outer, far = lax.optimization_barrier((outer, far))

    def inner_body(*refs):
        inner_kernel(*refs, unscale=1.0 / applied_scale)

    held = call(
        inner_body,
        jax.ShapeDtypeStruct((planes + 1, fields, ny, nz), F32),
        (mine, theirs, away, outer),
        [VMEM] * 4,
        VMEM,
    )
    inner = lax.ppermute(held, "slab", swap)
    devices = harmonics * slabs

    def chebyshev_body(*refs):
        chebyshev_kernel(*refs, unscale=1.0 / applied_scale)

    change, sums = call(
        chebyshev_body,
        [jax.ShapeDtypeStruct(shape, F32), jax.ShapeDtypeStruct((devices, 1, nz), F32)],
        (shifts, gram, basis, vec, mine, theirs, away, outer, inner, far),
        [SMEM] + [VMEM] * 9,
        [VMEM, VMEM],
    )
    sums = lax.all_to_all(sums, ("harm", "slab"), 0, 0, tiled=True)
    entries = float(devices * fields * planes * ny * nz)

    def final_body(*refs):
        final_kernel(*refs, entries=entries)

    vector, column = call(
        final_body,
        [jax.ShapeDtypeStruct((1,) + shape, F32), jax.ShapeDtypeStruct((count + 1,), F32)],
        (weights, basis, change, sums),
        [SMEM] + [VMEM] * 3,
        [VMEM, SMEM],
    )
    return vector, column


def solution(mesh):
    in_specs = (
        P(None, "harm", None, "slab", None, None),
        P(),
        P("harm", None, "slab", None, None),
        P("harm"),
    )
    out_specs = (P("harm", None, "slab", None, None), P())
    return jax.shard_map(shards, mesh=mesh, in_specs=in_specs, out_specs=out_specs, check_vma=False)
```

time: 200 us -> 39.3 us (0.20)
  blocking collectives: 151 us -> 11.4 us
  starting transfers between devices: 30.8 us -> 12.9 us
  other arithmetic: 4.62 us -> 0.14 us
  Pallas kernels: 0 us -> 4.28 us
  local copies, waits for them, and re-layouts: 4.36 us -> 1.21 us
    psum x6 -> x0, blocking collectives: 151 us -> none  [the longest x4 70 us: broadcast(): return lax.psum(jnp.where(mine, x, jnp.zeros_like(x)), axis)]
    ppermute x13 -> x7, starting transfers between devices: 30.8 us -> 12.9 us  [the longest x3 5.97 us: shards(): lax.ppermute(message, 'harm', [(i, (i + j) % harmonics) for i in range(ha...]
    all_to_all x0 -> x1, blocking collectives: none -> 11.4 us  [shards(): sums = lax.all_to_all(sums, ('harm', 'slab'), 0, 0, tiled=True)]
    pallas_call x0 -> x7, Pallas kernels: none -> 4.28 us  [call(): pl.pallas_call(body, out_shape=out_shape, in_specs=specs, out_specs=out_s...]
    ppermute x13 -> x7, waiting for transfers between devices: 5.94 us -> 7.62 us  [the longest x3 3.14 us: shards(): lax.ppermute(message, 'harm', [(i, (i + j) % harmonics) for i in range(ha...]
  transfers between devices with their start and end apart: 13 -> 7, of which waited for: 4 -> 6; matrix products, arithmetic and copies ran while one was open for 1% -> 0% of each run, Pallas kernels for 0% -> 1%
where the time goes in v1:
time: 39.3 us; the launch traced here: 39 us
  starting transfers between devices  12.9 us (33%)
  blocking collectives  11.4 us (29%)
  waiting for transfers between devices  7.62 us (19%)
  Pallas kernels  4.28 us (11%)
  between operations  1.41 us (4%)
  local copies, waits for them, and re-layouts  1.21 us (3%)
    all_to_all x1, blocking collectives, shards(): sums = lax.all_to_all(sums, ('harm', 'slab'), 0, 0, tiled=True)  11.4 us
    ppermute x3, starting transfers between devices, shards(): lax.ppermute(message, 'harm', [(i, (i + j) % harmonics) for i in range(ha...  5.97 us
    ppermute x1, starting transfers between devices, shards(): far = lax.ppermute(away_sent.astype(SENT), 'slab', beyond).astype(F32)  5.38 us
    pallas_call x7, Pallas kernels, call(): pl.pallas_call(body, out_shape=out_shape, in_specs=specs, out_specs=out_s...  4.28 us
    ppermute x3, waiting for transfers between devices, shards(): lax.ppermute(message, 'harm', [(i, (i + j) % harmonics) for i in range(ha...  3.14 us
    ppermute x1, waiting for transfers between devices, shards(): far = lax.ppermute(away_sent.astype(SENT), 'slab', beyond).astype(F32)  2.18 us
    ppermute x1, waiting for transfers between devices, shards(): theirs = lax.ppermute(mine, 'slab', swap)  1.43 us
    unnamed x4, local copies, waits for them, and re-layouts  1.21 us
  transfers between devices with their start and end apart: 7, of which 6 were waited for; matrix products, arithmetic and copies ran while one was open for 0% of the time, Pallas kernels for 1%

profile of v1, /device:TPU:0, one launch (start us, length us, event | category | flops | bytes accessed | tf_op | source)
XLA Modules:
  0.0 39.0 jit_solution(2584164607802726149)
XLA Ops:
  0.6 1.1 %shard_map.59 = (f32[3,1,4,2,32,128]{5,4,3,2,1,0:T(8,128)S(1)}, f32[4,2,32,128]{3,2,1,0:T(8,128)S(1)}, f32[7,2,32,128]{3,2,1,0:T(8,128)S(1)}) custom-call(f32[3,1,4,2,32,128]{5,4,3,2,1,0:T(8,128)} %refs_0_.4, f32[3]{0:T(128)} %refs_0_.5, bf16[1,3,2,32,128]{4,3,2,1,0:T(8,128)(2,1)} %refs_2_.1), custom_call_target="tpu_custom_call" | custom-call | tf_op jit(solution)/shard_map/pallas_call | solution.py:23
  1.8 3.0 %collective-permute-start = (f16[7,2,32,128]{3,2,1,0:T(8,128)(2,1)S(1)}, f16[7,2,32,128]{3,2,1,0:T(8,128)(2,1)S(1)}, u32[]{:S(2)}, u32[]{:S(2)}) collective-permute-start(f16[7,2,32,128]{3,2,1,0:T(8,128)(2,1)S(1)} %convert_element_type.24), channel_id=1, source_target_pairs={{0,8},{8,16},{16,24},{24,0},{1,9},{9,17},{17,25},{25,1},{2,10},{10... | collective-permute-start | bytes 344072 | tf_op jit(solution)/shard_map/ppermute | solution.py:309
  4.8 1.5 %collective-permute-start.1 = (f16[7,2,32,128]{3,2,1,0:T(8,128)(2,1)S(1)}, f16[7,2,32,128]{3,2,1,0:T(8,128)(2,1)S(1)}, u32[]{:S(2)}, u32[]{:S(2)}) collective-permute-start(f16[7,2,32,128]{3,2,1,0:T(8,128)(2,1)S(1)} %convert_element_type.24), channel_id=1, source_target_pairs={{0,16},{8,24},{16,0},{24,8},{1,17},{9,25},{17,1},{25,9},{2,18},{10... | collective-permute-start | bytes 344072 | tf_op jit(solution)/shard_map/ppermute | solution.py:309
  6.3 1.4 %collective-permute-start.2 = (f16[7,2,32,128]{3,2,1,0:T(8,128)(2,1)S(1)}, f16[7,2,32,128]{3,2,1,0:T(8,128)(2,1)S(1)}, u32[]{:S(2)}, u32[]{:S(2)}) collective-permute-start(f16[7,2,32,128]{3,2,1,0:T(8,128)(2,1)S(1)} %convert_element_type.24), channel_id=1, source_target_pairs={{0,24},{8,0},{16,8},{24,16},{1,25},{9,1},{17,9},{25,17},{2,26},{10... | collective-permute-start | bytes 344072 | tf_op jit(solution)/shard_map/ppermute | solution.py:309
  8.4 1.3 %collective-permute-done = f16[7,2,32,128]{3,2,1,0:T(8,128)(2,1)S(1)} collective-permute-done((f16[7,2,32,128]{3,2,1,0:T(8,128)(2,1)S(1)}, f16[7,2,32,128]{3,2,1,0:T(8,128)(2,1)S(1)}, u32[]{:S(2)}, u32[]{:S(2)}) %collective-permute-start) | collective-permute-done | bytes 114720 | tf_op jit(solution)/shard_map/ppermute | solution.py:309
  9.7 1.7 %collective-permute-done.1 = f16[7,2,32,128]{3,2,1,0:T(8,128)(2,1)S(1)} collective-permute-done((f16[7,2,32,128]{3,2,1,0:T(8,128)(2,1)S(1)}, f16[7,2,32,128]{3,2,1,0:T(8,128)(2,1)S(1)}, u32[]{:S(2)}, u32[]{:S(2)}) %collective-permute-start.1) | collective-permute-done | bytes 114720 | tf_op jit(solution)/shard_map/ppermute | solution.py:309
  11.4 0.0 copy-start
  11.4 0.2 collective-permute-done.2
  11.7 0.6 %copy-done = bf16[1,3,2,32,128]{4,3,2,1,0:T(8,128)(2,1)S(1)} copy-done((bf16[1,3,2,32,128]{4,3,2,1,0:T(8,128)(2,1)S(1)}, bf16[1,3,2,32,128]{4,3,2,1,0:T(8,128)(2,1)}, u32[]{:S(2)}) %copy-start) | copy-done | bytes 49176
  12.2 0.3 shard_map.61
  12.5 0.1 collective-permute-start.3
  12.6 1.4 %collective-permute-done.3.refs_1_.refs_5_ = f32[3,4,32,128]{3,2,1,0:T(8,128)S(1)} collective-permute-done((f32[3,4,32,128]{3,2,1,0:T(8,128)S(1)}, f32[3,4,32,128]{3,2,1,0:T(8,128)S(1)}, u32[]{:S(2)}, u32[]{:S(2)}) %collective-permute-start.3) | collective-permute-done | bytes 196640 | tf_op jit(solution)/shard_map/ppermute | solution.py:333
  14.1 0.7 %collective-permute-start.4 = (f16[5,4,32,128]{3,2,1,0:T(8,128)(2,1)S(1)}, f16[5,4,32,128]{3,2,1,0:T(8,128)(2,1)S(1)}, u32[]{:S(2)}, u32[]{:S(2)}) collective-permute-start(f16[5,4,32,128]{3,2,1,0:T(8,128)(2,1)S(1)} %convert_element_type.28), channel_id=1, source_target_pairs={{1,2},{3,4},{5,6},{2,1},{4,3},{6,5},{9,10},{11,12},{13,14},{10,9},... | collective-permute-start | bytes 491528 | tf_op jit(solution)/shard_map/ppermute | solution.py:345
  14.8 5.4 %collective-permute-start.5 = (f16[4,32,128]{2,1,0:T(8,128)(2,1)S(1)}, f16[4,32,128]{2,1,0:T(8,128)(2,1)S(1)}, u32[]{:S(2)}, u32[]{:S(2)}) collective-permute-start(f16[4,32,128]{2,1,0:T(8,128)(2,1)S(1)} %convert_element_type.30), channel_id=1, source_target_pairs={{0,5},{1,4},{2,7},{3,6},{4,1},{5,0},{6,3},{7,2},{8,13},{9,12},{10,... | collective-permute-start | bytes 98312 | tf_op jit(solution)/shard_map/ppermute | solution.py:349
  20.2 2.2 %collective-permute-done.5 = f16[4,32,128]{2,1,0:T(8,128)(2,1)S(1)} collective-permute-done((f16[4,32,128]{2,1,0:T(8,128)(2,1)S(1)}, f16[4,32,128]{2,1,0:T(8,128)(2,1)S(1)}, u32[]{:S(2)}, u32[]{:S(2)}) %collective-permute-start.5) | collective-permute-done | bytes 32800 | tf_op jit(solution)/shard_map/ppermute | solution.py:349
  22.3 0.0 collective-permute-done.4
  22.4 0.8 %collective-permute-start.6 = (f32[3,4,32,128]{3,2,1,0:T(8,128)S(1)}, f32[3,4,32,128]{3,2,1,0:T(8,128)S(1)}, u32[]{:S(2)}, u32[]{:S(2)}) collective-permute-start(f32[3,4,32,128]{3,2,1,0:T(8,128)S(1)} %shard_map.63), channel_id=1, source_target_pairs={{0,1},{1,0},{2,3},{3,2},{4,5},{5,4},{6,7},{7,6},{8,9},{9,8},{10,11... | collective-permute-start | bytes 589832 | tf_op jit(solution)/shard_map/ppermute | solution.py:363
  23.3 0.2 shard_map.60.refs_1_
  23.5 0.9 %collective-permute-done.6.refs_8_ = f32[3,4,32,128]{3,2,1,0:T(8,128)S(1)} collective-permute-done((f32[3,4,32,128]{3,2,1,0:T(8,128)S(1)}, f32[3,4,32,128]{3,2,1,0:T(8,128)S(1)}, u32[]{:S(2)}, u32[]{:S(2)}) %collective-permute-start.6) | collective-permute-done | bytes 196640 | tf_op jit(solution)/shard_map/ppermute | solution.py:363
  24.3 1.2 %shard_map.64 = (f32[4,2,32,128]{3,2,1,0:T(8,128)S(1)}, f32[32,1,128]{2,1,0:T(1,128)S(1)}) custom-call(f32[1]{0:T(128)S(6)} %copy.6.refs_0_, f32[1,128]{1,0:T(1,128)S(1)} %shard_map.60.refs_1_, f32[3,1,4,2,32,128]{5,4,3,2,1,0:T(8,128)S(1)} %get-tuple-element.12.basis.refs_2_.refs_1_, f32[4,2,32,128]{3,2,1,0:T(8,128)S(1)} %get-tuple-element.13.refs_1_.refs_3_, ...), custom_call_target="tpu_custom_call" | custom-call | tf_op jit(solution)/shard_map/pallas_call | solution.py:23
  25.5 11.4 %all_to_all.5.refs_3_ = f32[32,1,128]{2,1,0:T(1,128)S(1)} all-to-all(f32[32,1,128]{2,1,0:T(1,128)S(1)} %get-tuple-element.21), channel_id=1, replica_groups=mesh['harm'=4,'slab'=8] {'harm','slab'}, dimensions={0} | all-to-all | bytes 32768 | tf_op jit(solution)/shard_map/all_to_all | solution.py:376
  37.0 0.0 copy-start.1
  37.0 0.7 %copy-done.1 = f32[3]{0:T(128)S(1)} copy-done((f32[3]{0:T(128)S(1)}, f32[3]{0:T(128)}, u32[]{:S(2)}) %copy-start.1) | copy-done | bytes 36
  37.6 1.4 %shard_map.65 = (f32[1,4,2,32,128]{4,3,2,1,0:T(8,128)}, f32[4]{0:T(128)}) custom-call(f32[3]{0:T(128)S(1)} %copy-done.1, f32[3,1,4,2,32,128]{5,4,3,2,1,0:T(8,128)S(1)} %get-tuple-element.12.basis.refs_2_.refs_1_, f32[4,2,32,128]{3,2,1,0:T(8,128)S(1)} %get-tuple-element.20.refs_2_, f32[32,1,128]{2,1,0:T(1,128)S(1)} %all_to_all.5.refs_3_), custom_call_target="tpu_custom_call" | custom-call | tf_op jit(solution)/shard_map/pallas_call | solution.py:23
  (10 shorter events, 0.2 us)
Async XLA Ops:
  1.8 7.9 %collective-permute-start = (f16[7,2,32,128]{3,2,1,0:T(8,128)(2,1)S(1)}, f16[7,2,32,128]{3,2,1,0:T(8,128)(2,1)S(1)}, u32[]{:S(2)}, u32[]{:S(2)}) collective-permute-start(f16[7,2,32,128]{3,2,1,0:T(8,128)(2,1)S(1)} %convert_element_type.24), channel_id=1, source_target_pairs={{0,8},{8,16},{16,24},{24,0},{1,9},{9,17},{17,25},{25,1},{2,10},{10... | collective-permute-start | bytes 344072 | tf_op jit(solution)/shard_map/ppermute | solution.py:309
  4.8 6.6 %collective-permute-start.1 = (f16[7,2,32,128]{3,2,1,0:T(8,128)(2,1)S(1)}, f16[7,2,32,128]{3,2,1,0:T(8,128)(2,1)S(1)}, u32[]{:S(2)}, u32[]{:S(2)}) collective-permute-start(f16[7,2,32,128]{3,2,1,0:T(8,128)(2,1)S(1)} %convert_element_type.24), channel_id=1, source_target_pairs={{0,16},{8,24},{16,0},{24,8},{1,17},{9,25},{17,1},{25,9},{2,18},{10... | collective-permute-start | bytes 344072 | tf_op jit(solution)/shard_map/ppermute | solution.py:309
  6.3 5.3 %collective-permute-start.2 = (f16[7,2,32,128]{3,2,1,0:T(8,128)(2,1)S(1)}, f16[7,2,32,128]{3,2,1,0:T(8,128)(2,1)S(1)}, u32[]{:S(2)}, u32[]{:S(2)}) collective-permute-start(f16[7,2,32,128]{3,2,1,0:T(8,128)(2,1)S(1)} %convert_element_type.24), channel_id=1, source_target_pairs={{0,24},{8,0},{16,8},{24,16},{1,25},{9,1},{17,9},{25,17},{2,26},{10... | collective-permute-start | bytes 344072 | tf_op jit(solution)/shard_map/ppermute | solution.py:309
  11.4 0.8 %copy-start = (bf16[1,3,2,32,128]{4,3,2,1,0:T(8,128)(2,1)S(1)}, bf16[1,3,2,32,128]{4,3,2,1,0:T(8,128)(2,1)}, u32[]{:S(2)}) copy-start(bf16[1,3,2,32,128]{4,3,2,1,0:T(8,128)(2,1)} %refs_2_.1) | copy-start | bytes 147460
  12.5 1.5 %collective-permute-start.3 = (f32[3,4,32,128]{3,2,1,0:T(8,128)S(1)}, f32[3,4,32,128]{3,2,1,0:T(8,128)S(1)}, u32[]{:S(2)}, u32[]{:S(2)}) collective-permute-start(f32[3,4,32,128]{3,2,1,0:T(8,128)S(1)} %get-tuple-element.15.refs_0_.refs_4_), channel_id=1, source_target_pairs={{0,1},{1,0},{2,3},{3,2},{4,5},{5,4},{6,7},{7,6},{8,9},{9,8},{10,11... | collective-permute-start | bytes 589832 | tf_op jit(solution)/shard_map/ppermute | solution.py:333
  14.1 8.3 %collective-permute-start.4 = (f16[5,4,32,128]{3,2,1,0:T(8,128)(2,1)S(1)}, f16[5,4,32,128]{3,2,1,0:T(8,128)(2,1)S(1)}, u32[]{:S(2)}, u32[]{:S(2)}) collective-permute-start(f16[5,4,32,128]{3,2,1,0:T(8,128)(2,1)S(1)} %convert_element_type.28), channel_id=1, source_target_pairs={{1,2},{3,4},{5,6},{2,1},{4,3},{6,5},{9,10},{11,12},{13,14},{10,9},... | collective-permute-start | bytes 491528 | tf_op jit(solution)/shard_map/ppermute | solution.py:345
  14.8 7.6 %collective-permute-start.5 = (f16[4,32,128]{2,1,0:T(8,128)(2,1)S(1)}, f16[4,32,128]{2,1,0:T(8,128)(2,1)S(1)}, u32[]{:S(2)}, u32[]{:S(2)}) collective-permute-start(f16[4,32,128]{2,1,0:T(8,128)(2,1)S(1)} %convert_element_type.30), channel_id=1, source_target_pairs={{0,5},{1,4},{2,7},{3,6},{4,1},{5,0},{6,3},{7,2},{8,13},{9,12},{10,... | collective-permute-start | bytes 98312 | tf_op jit(solution)/shard_map/ppermute | solution.py:349
  22.4 1.9 %collective-permute-start.6 = (f32[3,4,32,128]{3,2,1,0:T(8,128)S(1)}, f32[3,4,32,128]{3,2,1,0:T(8,128)S(1)}, u32[]{:S(2)}, u32[]{:S(2)}) collective-permute-start(f32[3,4,32,128]{3,2,1,0:T(8,128)S(1)} %shard_map.63), channel_id=1, source_target_pairs={{0,1},{1,0},{2,3},{3,2},{4,5},{5,4},{6,7},{7,6},{8,9},{9,8},{10,11... | collective-permute-start | bytes 589832 | tf_op jit(solution)/shard_map/ppermute | solution.py:363
  37.0 0.7 %copy-start.1 = (f32[3]{0:T(128)S(1)}, f32[3]{0:T(128)}, u32[]{:S(2)}) copy-start(f32[3]{0:T(128)} %refs_0_.5) | copy-start | bytes 40

commit v2 on v1

--- a/solution.py
+++ b/solution.py
@@ -58,7 +58,7 @@
     return [2.0 ** math.floor(math.log2(SENT_MAX / bound)) for bound in (vector, applied)]
 
 
-def start_kernel(basis_in, weights_in, flow_in, basis, vec, message, weights, flow, sems, *, rescale):
+def start_kernel(basis_in, weights_in, flow_in, basis, vec, message, scalars, weights, flow, sems, *, rescale):
     count, fields = basis.shape[0], basis.shape[2]
     copies = [pltpu.make_async_copy(weights_in, weights, sems.at[0])]
     copies.append(pltpu.make_async_copy(flow_in, flow, sems.at[1]))
@@ -74,6 +74,8 @@
         vec[f] = total
         message[f] = total * rescale
     message[fields:] = flow[0].astype(F32)
+    for j in range(count):
+        scalars[j : j + 1] = jnp.full((1, scalars.shape[1]), weights[j], F32)
 
 
 def gram_kernel(basis, sums):
@@ -96,9 +98,8 @@
     sign = 0.5 * (1 - 2 * core).astype(F32)
     flip = core == 1
     for j in range(harmonics):
-        flow = messages[0][...].astype(F32) if j == 0 else messages[j][fields:]
-        flows[lax.rem(harm - j + harmonics, harmonics)] = flow
-    own = shift[0] + 6.0 * VISCOSITY
+        flows[lax.rem(harm - j + harmonics, harmonics)] = messages[j][fields:]
+    own = shift[...] + 6.0 * VISCOSITY
     for f in range(fields):
         local, plus, minus = [], [], []
         for t in range(planes):
@@ -165,7 +166,7 @@
     has_inner = jnp.where(flip, has_low, has_high)
     two_away = jnp.where(flip, chips - 1 - chip, chip) > 1
     has_far = two_away.astype(F32)
-    own_shift = shift[0]
+    own_shift = shift[...]
     middle = own_shift + 6.0 * VISCOSITY
     half_span = 6.0 * VISCOSITY
     span_ratio = middle / half_span
@@ -239,13 +240,13 @@
     sums[...] = jnp.broadcast_to(line[None], sums.shape)
 
 
-def final_kernel(weights, basis, change, sums, vector, column, *, entries):
+def final_kernel(scalars, basis, change, sums, vector, column, *, entries):
     count = basis.shape[0]
     line = jnp.sum(sums[:, 0, :], axis=0, keepdims=True) * (1.0 / entries)
     lanes = lax.broadcasted_iota(jnp.int32, line.shape, 1)
 
     def entry(place):
-        return jnp.sum(jnp.where(lanes == place, line, 0.0))
+        return jnp.sum(jnp.where(lanes == place, line, 0.0), axis=1, keepdims=True)
 
     square = entry(0)
     moved = [entry(1 + j) for j in range(count)]
@@ -254,6 +255,7 @@
         for j in range(i, count):
             gram[i, j] = gram[j, i] = entry(place)
             place += 1
+    weights = [scalars[j : j + 1] for j in range(count)]
     projection, excess = [], []
     for j in range(count):
         value = moved[j]
@@ -266,14 +268,14 @@
         for i in range(count):
             inner = inner + excess[i] * gram[i, j]
         square = square + excess[j] * inner
-    norm = jnp.sqrt(jnp.full((1, line.shape[-1]), jnp.maximum(square, 0.0) + EPSILON, F32))
+    norm = jnp.sqrt(jnp.maximum(square, 0.0) + EPSILON)
     inverse = (1.0 / norm)[:, None, None, :]
     residue = change[...]
     for j in range(count):
-        residue = residue - excess[j] * basis[j, 0]
+        residue = residue - excess[j][:, None, None, :] * basis[j, 0]
     vector[0] = residue * inverse
     for j in range(count):
-        column[j] = projection[j]
+        column[j] = jnp.max(projection[j])
     column[count] = jnp.max(norm)
 
 
@@ -287,25 +289,27 @@
     def start_body(*refs):
         start_kernel(*refs, rescale=vec_scale)
 
-    basis, vec, message = call(
+    basis, vec, message, scalars = call(
         start_body,
         [
             jax.ShapeDtypeStruct(krylov_basis.shape, F32),
             jax.ShapeDtypeStruct(shape, F32),
             jax.ShapeDtypeStruct((fields + DIRS, planes, ny, nz), F32),
+            jax.ShapeDtypeStruct((count, nz), F32),
         ],
-        [pltpu.with_memory_space_constraint(x, pltpu.HBM) for x in (krylov_basis, weights, base_flow)],
+        [*(pltpu.with_memory_space_constraint(x, pltpu.HBM) for x in (krylov_basis, weights, base_flow))],
         [pl.BlockSpec(memory_space=pltpu.HBM)] * 3,
-        [VMEM] * 3,
+        [VMEM] * 4,
         [
             pltpu.SMEM(weights.shape, F32),
             pltpu.VMEM(base_flow.shape, base_flow.dtype),
             pltpu.SemaphoreType.DMA((2 + count,)),
         ],
     )
-    message = message.astype(SENT)
+    whole, message = message, message.astype(SENT)
+    shift = jnp.broadcast_to(shifts[:, None], (1, nz))
     gram = call(gram_kernel, jax.ShapeDtypeStruct((1, nz), F32), (basis,), [VMEM], VMEM)
-    messages = [base_flow[0]] + [
+    messages = [whole] + [
         lax.ppermute(message, "harm", [(i, (i + j) % harmonics) for i in range(harmonics)]).astype(F32)
         for j in range(1, harmonics)
     ]
@@ -320,8 +324,8 @@
             jax.ShapeDtypeStruct((fields, ny, nz), F32),
             jax.ShapeDtypeStruct((fields, ny, nz), F32),
         ],
-        (shifts, vec, *messages),
-        [SMEM] + [VMEM] * (1 + harmonics),
+        (shift, vec, *messages),
+        [VMEM] * (2 + harmonics),
         [VMEM] * 3,
         [pltpu.VMEM((harmonics, DIRS, planes, ny, nz), F32)],
     )
@@ -369,8 +373,8 @@
     change, sums = call(
         chebyshev_body,
         [jax.ShapeDtypeStruct(shape, F32), jax.ShapeDtypeStruct((devices, 1, nz), F32)],
-        (shifts, gram, basis, vec, mine, theirs, away, outer, inner, far),
-        [SMEM] + [VMEM] * 9,
+        (shift, gram, basis, vec, mine, theirs, away, outer, inner, far),
+        [VMEM] * 10,
         [VMEM, VMEM],
     )
     sums = lax.all_to_all(sums, ("harm", "slab"), 0, 0, tiled=True)
@@ -382,8 +386,8 @@
     vector, column = call(
         final_body,
         [jax.ShapeDtypeStruct((1,) + shape, F32), jax.ShapeDtypeStruct((count + 1,), F32)],
-        (weights, basis, change, sums),
-        [SMEM] + [VMEM] * 3,
+        (scalars, basis, change, sums),
+        [VMEM] * 4,
         [VMEM, SMEM],
     )
     return vector, column

time: 39.3 us -> 37.2 us (0.947)
  local copies, waits for them, and re-layouts: 1.21 us -> 0.01 us
  Pallas kernels: 4.28 us -> 3.69 us
    unnamed x4 -> x0, local copies, waits for them, and re-layouts: 1.21 us -> none
    pallas_call x7, Pallas kernels: 4.28 us -> 3.69 us  [call(): pl.pallas_call(body, out_shape=out_shape, in_specs=specs, out_specs=out_s...]
where the time goes in v2:
time: 37.2 us; the launch traced here: 37 us
  starting transfers between devices  12.6 us (34%)
  blocking collectives  11.4 us (31%)
  waiting for transfers between devices  7.74 us (21%)
  Pallas kernels  3.69 us (10%)
  between operations  1.4 us (4%)
    all_to_all x1, blocking collectives, shards(): sums = lax.all_to_all(sums, ('harm', 'slab'), 0, 0, tiled=True)  11.4 us
    ppermute x3, starting transfers between devices, shards(): lax.ppermute(message, 'harm', [(i, (i + j) % harmonics) for i in range(ha...  5.97 us
    ppermute x1, starting transfers between devices, shards(): far = lax.ppermute(away_sent.astype(SENT), 'slab', beyond).astype(F32)  5.19 us
    pallas_call x7, Pallas kernels, call(): pl.pallas_call(body, out_shape=out_shape, in_specs=specs, out_specs=out_s...  3.69 us
    ppermute x3, waiting for transfers between devices, shards(): lax.ppermute(message, 'harm', [(i, (i + j) % harmonics) for i in range(ha...  3.16 us
    ppermute x1, waiting for transfers between devices, shards(): far = lax.ppermute(away_sent.astype(SENT), 'slab', beyond).astype(F32)  2.29 us
    ppermute x1, waiting for transfers between devices, shards(): theirs = lax.ppermute(mine, 'slab', swap)  1.43 us
    ppermute x1, waiting for transfers between devices, shards(): inner = lax.ppermute(held, 'slab', swap)  0.86 us
  transfers between devices with their start and end apart: 7, of which 6 were waited for; matrix products, arithmetic and copies ran while one was open for 0% of the time, Pallas kernels for 1%

profile of v2, /device:TPU:0, one launch (start us, length us, event | category | flops | bytes accessed | tf_op | source)
XLA Modules:
  0.0 37.0 jit_solution(8179461434544296925)
XLA Ops:
  0.6 1.1 %shard_map.59 = (f32[3,1,4,2,32,128]{5,4,3,2,1,0:T(8,128)S(1)}, f32[4,2,32,128]{3,2,1,0:T(8,128)S(1)}, f32[7,2,32,128]{3,2,1,0:T(8,128)S(1)}, f32[3,128]{1,0:T(4,128)S(1)}) custom-call(f32[3,1,4,2,32,128]{5,4,3,2,1,0:T(8,128)} %refs_0_.1, f32[3]{0:T(128)} %refs_1_.1, bf16[1,3,2,32,128]{4,3,2,1,0:T(8,128)(2,1)} %refs_2_.1), custom_call_target="tpu_custom_call" | custom-call | tf_op jit(solution)/shard_map/pallas_call | solution.py:23
  1.8 3.0 %collective-permute-start = (f16[7,2,32,128]{3,2,1,0:T(8,128)(2,1)S(1)}, f16[7,2,32,128]{3,2,1,0:T(8,128)(2,1)S(1)}, u32[]{:S(2)}, u32[]{:S(2)}) collective-permute-start(f16[7,2,32,128]{3,2,1,0:T(8,128)(2,1)S(1)} %convert_element_type.24), channel_id=1, source_target_pairs={{0,8},{8,16},{16,24},{24,0},{1,9},{9,17},{17,25},{25,1},{2,10},{10... | collective-permute-start | bytes 344072 | tf_op jit(solution)/shard_map/ppermute | solution.py:313
  4.8 1.5 %collective-permute-start.1 = (f16[7,2,32,128]{3,2,1,0:T(8,128)(2,1)S(1)}, f16[7,2,32,128]{3,2,1,0:T(8,128)(2,1)S(1)}, u32[]{:S(2)}, u32[]{:S(2)}) collective-permute-start(f16[7,2,32,128]{3,2,1,0:T(8,128)(2,1)S(1)} %convert_element_type.24), channel_id=1, source_target_pairs={{0,16},{8,24},{16,0},{24,8},{1,17},{9,25},{17,1},{25,9},{2,18},{10... | collective-permute-start | bytes 344072 | tf_op jit(solution)/shard_map/ppermute | solution.py:313
  6.3 1.4 %collective-permute-start.2 = (f16[7,2,32,128]{3,2,1,0:T(8,128)(2,1)S(1)}, f16[7,2,32,128]{3,2,1,0:T(8,128)(2,1)S(1)}, u32[]{:S(2)}, u32[]{:S(2)}) collective-permute-start(f16[7,2,32,128]{3,2,1,0:T(8,128)(2,1)S(1)} %convert_element_type.24), channel_id=1, source_target_pairs={{0,24},{8,0},{16,8},{24,16},{1,25},{9,1},{17,9},{25,17},{2,26},{10... | collective-permute-start | bytes 344072 | tf_op jit(solution)/shard_map/ppermute | solution.py:313
  8.4 1.3 %collective-permute-done = f16[7,2,32,128]{3,2,1,0:T(8,128)(2,1)S(1)} collective-permute-done((f16[7,2,32,128]{3,2,1,0:T(8,128)(2,1)S(1)}, f16[7,2,32,128]{3,2,1,0:T(8,128)(2,1)S(1)}, u32[]{:S(2)}, u32[]{:S(2)}) %collective-permute-start) | collective-permute-done | bytes 114720 | tf_op jit(solution)/shard_map/ppermute | solution.py:313
  9.7 1.7 %collective-permute-done.1 = f16[7,2,32,128]{3,2,1,0:T(8,128)(2,1)S(1)} collective-permute-done((f16[7,2,32,128]{3,2,1,0:T(8,128)(2,1)S(1)}, f16[7,2,32,128]{3,2,1,0:T(8,128)(2,1)S(1)}, u32[]{:S(2)}, u32[]{:S(2)}) %collective-permute-start.1) | collective-permute-done | bytes 114720 | tf_op jit(solution)/shard_map/ppermute | solution.py:313
  11.4 0.2 collective-permute-done.2
  11.7 0.3 shard_map.61
  12.0 0.1 collective-permute-start.3
  12.1 1.4 %collective-permute-done.3.refs_1_.refs_5_ = f32[3,4,32,128]{3,2,1,0:T(8,128)S(1)} collective-permute-done((f32[3,4,32,128]{3,2,1,0:T(8,128)S(1)}, f32[3,4,32,128]{3,2,1,0:T(8,128)S(1)}, u32[]{:S(2)}, u32[]{:S(2)}) %collective-permute-start.3) | collective-permute-done | bytes 196640 | tf_op jit(solution)/shard_map/ppermute | solution.py:337
  13.5 0.7 %collective-permute-start.4 = (f16[5,4,32,128]{3,2,1,0:T(8,128)(2,1)S(1)}, f16[5,4,32,128]{3,2,1,0:T(8,128)(2,1)S(1)}, u32[]{:S(2)}, u32[]{:S(2)}) collective-permute-start(f16[5,4,32,128]{3,2,1,0:T(8,128)(2,1)S(1)} %convert_element_type.28), channel_id=1, source_target_pairs={{1,2},{3,4},{5,6},{2,1},{4,3},{6,5},{9,10},{11,12},{13,14},{10,9},... | collective-permute-start | bytes 491528 | tf_op jit(solution)/shard_map/ppermute | solution.py:349
  14.2 5.2 %collective-permute-start.5 = (f16[4,32,128]{2,1,0:T(8,128)(2,1)S(1)}, f16[4,32,128]{2,1,0:T(8,128)(2,1)S(1)}, u32[]{:S(2)}, u32[]{:S(2)}) collective-permute-start(f16[4,32,128]{2,1,0:T(8,128)(2,1)S(1)} %convert_element_type.30), channel_id=1, source_target_pairs={{0,5},{1,4},{2,7},{3,6},{4,1},{5,0},{6,3},{7,2},{8,13},{9,12},{10,... | collective-permute-start | bytes 98312 | tf_op jit(solution)/shard_map/ppermute | solution.py:353
  19.4 2.3 %collective-permute-done.5 = f16[4,32,128]{2,1,0:T(8,128)(2,1)S(1)} collective-permute-done((f16[4,32,128]{2,1,0:T(8,128)(2,1)S(1)}, f16[4,32,128]{2,1,0:T(8,128)(2,1)S(1)}, u32[]{:S(2)}, u32[]{:S(2)}) %collective-permute-start.5) | collective-permute-done | bytes 32800 | tf_op jit(solution)/shard_map/ppermute | solution.py:353
  21.7 0.0 collective-permute-done.4
  21.8 0.7 %collective-permute-start.6 = (f32[3,4,32,128]{3,2,1,0:T(8,128)S(1)}, f32[3,4,32,128]{3,2,1,0:T(8,128)S(1)}, u32[]{:S(2)}, u32[]{:S(2)}) collective-permute-start(f32[3,4,32,128]{3,2,1,0:T(8,128)S(1)} %shard_map.63), channel_id=1, source_target_pairs={{0,1},{1,0},{2,3},{3,2},{4,5},{5,4},{6,7},{7,6},{8,9},{9,8},{10,11... | collective-permute-start | bytes 589832 | tf_op jit(solution)/shard_map/ppermute | solution.py:367
  22.5 0.2 shard_map.60.refs_1_
  22.7 0.9 %collective-permute-done.6.refs_8_ = f32[3,4,32,128]{3,2,1,0:T(8,128)S(1)} collective-permute-done((f32[3,4,32,128]{3,2,1,0:T(8,128)S(1)}, f32[3,4,32,128]{3,2,1,0:T(8,128)S(1)}, u32[]{:S(2)}, u32[]{:S(2)}) %collective-permute-start.6) | collective-permute-done | bytes 196640 | tf_op jit(solution)/shard_map/ppermute | solution.py:367
  23.6 1.2 %shard_map.64 = (f32[4,2,32,128]{3,2,1,0:T(8,128)S(1)}, f32[32,1,128]{2,1,0:T(1,128)S(1)}) custom-call(f32[1,128]{1,0:T(1,128)S(1)} %broadcast_in_dim.9.refs_0_, f32[1,128]{1,0:T(1,128)S(1)} %shard_map.60.refs_1_, f32[3,1,4,2,32,128]{5,4,3,2,1,0:T(8,128)S(1)} %get-tuple-element.14.basis.refs_2_.refs_1_, ...), custom_call_target="tpu_custom_call" | custom-call | tf_op jit(solution)/shard_map/pallas_call | solution.py:23
  24.8 11.4 %all_to_all.5.refs_3_ = f32[32,1,128]{2,1,0:T(1,128)S(1)} all-to-all(f32[32,1,128]{2,1,0:T(1,128)S(1)} %get-tuple-element.23), channel_id=1, replica_groups=mesh['harm'=4,'slab'=8] {'harm','slab'}, dimensions={0} | all-to-all | bytes 32768 | tf_op jit(solution)/shard_map/all_to_all | solution.py:380
  36.2 0.8 %shard_map.65 = (f32[1,4,2,32,128]{4,3,2,1,0:T(8,128)}, f32[4]{0:T(128)}) custom-call(f32[3,128]{1,0:T(4,128)S(1)} %get-tuple-element.13.refs_0_, f32[3,1,4,2,32,128]{5,4,3,2,1,0:T(8,128)S(1)} %get-tuple-element.14.basis.refs_2_.refs_1_, f32[4,2,32,128]{3,2,1,0:T(8,128)S(1)} %get-tuple-element.22.refs_2_, f32[32,1,128]{2,1,0:T(1,128)S(1)} %all_to_all.5.refs_3_), custom_call_target="tpu_custom_call" | custom-call | tf_op jit(solution)/shard_map/pallas_call | solution.py:23
  (11 shorter events, 0.2 us)
Async XLA Ops:
  1.8 7.9 %collective-permute-start = (f16[7,2,32,128]{3,2,1,0:T(8,128)(2,1)S(1)}, f16[7,2,32,128]{3,2,1,0:T(8,128)(2,1)S(1)}, u32[]{:S(2)}, u32[]{:S(2)}) collective-permute-start(f16[7,2,32,128]{3,2,1,0:T(8,128)(2,1)S(1)} %convert_element_type.24), channel_id=1, source_target_pairs={{0,8},{8,16},{16,24},{24,0},{1,9},{9,17},{17,25},{25,1},{2,10},{10... | collective-permute-start | bytes 344072 | tf_op jit(solution)/shard_map/ppermute | solution.py:313
  4.8 6.6 %collective-permute-start.1 = (f16[7,2,32,128]{3,2,1,0:T(8,128)(2,1)S(1)}, f16[7,2,32,128]{3,2,1,0:T(8,128)(2,1)S(1)}, u32[]{:S(2)}, u32[]{:S(2)}) collective-permute-start(f16[7,2,32,128]{3,2,1,0:T(8,128)(2,1)S(1)} %convert_element_type.24), channel_id=1, source_target_pairs={{0,16},{8,24},{16,0},{24,8},{1,17},{9,25},{17,1},{25,9},{2,18},{10... | collective-permute-start | bytes 344072 | tf_op jit(solution)/shard_map/ppermute | solution.py:313
  6.3 5.3 %collective-permute-start.2 = (f16[7,2,32,128]{3,2,1,0:T(8,128)(2,1)S(1)}, f16[7,2,32,128]{3,2,1,0:T(8,128)(2,1)S(1)}, u32[]{:S(2)}, u32[]{:S(2)}) collective-permute-start(f16[7,2,32,128]{3,2,1,0:T(8,128)(2,1)S(1)} %convert_element_type.24), channel_id=1, source_target_pairs={{0,24},{8,0},{16,8},{24,16},{1,25},{9,1},{17,9},{25,17},{2,26},{10... | collective-permute-start | bytes 344072 | tf_op jit(solution)/shard_map/ppermute | solution.py:313
  12.0 1.5 %collective-permute-start.3 = (f32[3,4,32,128]{3,2,1,0:T(8,128)S(1)}, f32[3,4,32,128]{3,2,1,0:T(8,128)S(1)}, u32[]{:S(2)}, u32[]{:S(2)}) collective-permute-start(f32[3,4,32,128]{3,2,1,0:T(8,128)S(1)} %get-tuple-element.17.refs_0_.refs_4_), channel_id=1, source_target_pairs={{0,1},{1,0},{2,3},{3,2},{4,5},{5,4},{6,7},{7,6},{8,9},{9,8},{10,11... | collective-permute-start | bytes 589832 | tf_op jit(solution)/shard_map/ppermute | solution.py:337
  13.5 8.2 %collective-permute-start.4 = (f16[5,4,32,128]{3,2,1,0:T(8,128)(2,1)S(1)}, f16[5,4,32,128]{3,2,1,0:T(8,128)(2,1)S(1)}, u32[]{:S(2)}, u32[]{:S(2)}) collective-permute-start(f16[5,4,32,128]{3,2,1,0:T(8,128)(2,1)S(1)} %convert_element_type.28), channel_id=1, source_target_pairs={{1,2},{3,4},{5,6},{2,1},{4,3},{6,5},{9,10},{11,12},{13,14},{10,9},... | collective-permute-start | bytes 491528 | tf_op jit(solution)/shard_map/ppermute | solution.py:349
  14.2 7.5 %collective-permute-start.5 = (f16[4,32,128]{2,1,0:T(8,128)(2,1)S(1)}, f16[4,32,128]{2,1,0:T(8,128)(2,1)S(1)}, u32[]{:S(2)}, u32[]{:S(2)}) collective-permute-start(f16[4,32,128]{2,1,0:T(8,128)(2,1)S(1)} %convert_element_type.30), channel_id=1, source_target_pairs={{0,5},{1,4},{2,7},{3,6},{4,1},{5,0},{6,3},{7,2},{8,13},{9,12},{10,... | collective-permute-start | bytes 98312 | tf_op jit(solution)/shard_map/ppermute | solution.py:353
  21.8 1.8 %collective-permute-start.6 = (f32[3,4,32,128]{3,2,1,0:T(8,128)S(1)}, f32[3,4,32,128]{3,2,1,0:T(8,128)S(1)}, u32[]{:S(2)}, u32[]{:S(2)}) collective-permute-start(f32[3,4,32,128]{3,2,1,0:T(8,128)S(1)} %shard_map.63), channel_id=1, source_target_pairs={{0,1},{1,0},{2,3},{3,2},{4,5},{5,4},{6,7},{7,6},{8,9},{9,8},{10,11... | collective-permute-start | bytes 589832 | tf_op jit(solution)/shard_map/ppermute | solution.py:367

commit v3 on v2

--- a/solution.py
+++ b/solution.py
@@ -6,6 +6,7 @@
 from jax.experimental import pallas as pl
 from jax.experimental.pallas import tpu as pltpu
 from jax.sharding import PartitionSpec as P
+
 
 SWEEPS = 4
 DIRS = 3
@@ -49,6 +50,18 @@
 
 def parity():
     return lax.rem(lax.axis_index("slab"), 2)
+
+
+def step(index, j, harmonics):
+    if harmonics & (harmonics - 1) == 0:
+        return index ^ j
+    return (index + j) % harmonics
+
+
+def step_back(index, j, harmonics):
+    if harmonics & (harmonics - 1) == 0:
+        return lax.bitwise_xor(index, j)
+    return lax.rem(index - j + harmonics, harmonics)
 
 
 def scales(count, harmonics):
@@ -98,7 +111,7 @@
     sign = 0.5 * (1 - 2 * core).astype(F32)
     flip = core == 1
     for j in range(harmonics):
-        flows[lax.rem(harm - j + harmonics, harmonics)] = messages[j][fields:]
+        flows[step_back(harm, j, harmonics)] = messages[j][fields:]
     own = shift[...] + 6.0 * VISCOSITY
     for f in range(fields):
         local, plus, minus = [], [], []
@@ -108,7 +121,8 @@
             flux = [flows[0, d, x] * center for d in range(DIRS)]
             for j in range(1, harmonics):
                 other = messages[j][f, x] * unscale
-                flux = [flux[d] + flows[j, d, x] * other for d in range(DIRS)]
+                row = lax.rem(harm - step_back(harm, j, harmonics) + harmonics, harmonics)
+                flux = [flux[d] + flows[row, d, x] * other for d in range(DIRS)]
             half_y = 0.5 * flux[1]
             half_z = 0.5 * flux[2]
             half_x = sign * flux[0]
@@ -310,7 +324,7 @@
     shift = jnp.broadcast_to(shifts[:, None], (1, nz))
     gram = call(gram_kernel, jax.ShapeDtypeStruct((1, nz), F32), (basis,), [VMEM], VMEM)
     messages = [whole] + [
-        lax.ppermute(message, "harm", [(i, (i + j) % harmonics) for i in range(harmonics)]).astype(F32)
+        lax.ppermute(message, "harm", [(i, step(i, j, harmonics)) for i in range(harmonics)]).astype(F32)
         for j in range(1, harmonics)
     ]
 
@@ -352,8 +366,6 @@
         beyond = [(i, i ^ mask) for i in range(slabs) for mask in masks]
     far = lax.ppermute(away_sent.astype(SENT), "slab", beyond).astype(F32)
 
-    outer, far = lax.optimization_barrier((outer, far))
-
     def inner_body(*refs):
         inner_kernel(*refs, unscale=1.0 / applied_scale)
 
@@ -401,4 +413,5 @@
         P("harm"),
     )
     out_specs = (P("harm", None, "slab", None, None), P())
+
     return jax.shard_map(shards, mesh=mesh, in_specs=in_specs, out_specs=out_specs, check_vma=False)

time: 37.2 us -> 39.9 us (1.073)
  starting transfers between devices: 12.6 us -> 14.1 us
  blocking collectives: 11.4 us -> 12.4 us
    ppermute x1, starting transfers between devices: 0.74 us -> 6.15 us  [shards(): inner = lax.ppermute(held, 'slab', swap)]
    ppermute x1, starting transfers between devices: 5.19 us -> 2.63 us  [shards(): far = lax.ppermute(away_sent.astype(SENT), 'slab', beyond).astype(F32)]
    ppermute x3, waiting for transfers between devices: 3.16 us -> 5.04 us  [shards(): lax.ppermute(message, 'harm', [(i, step(i, j, harmonics)) for i in range(...]
    ppermute x3, starting transfers between devices: 5.97 us -> 4.57 us  [shards(): lax.ppermute(message, 'harm', [(i, step(i, j, harmonics)) for i in range(...]
    all_to_all x1, blocking collectives: 11.4 us -> 12.4 us  [shards(): sums = lax.all_to_all(sums, ('harm', 'slab'), 0, 0, tiled=True)]
    ppermute x1, waiting for transfers between devices: 0.86 us -> 0.01 us  [shards(): inner = lax.ppermute(held, 'slab', swap)]
    ppermute x1, waiting for transfers between devices: 2.29 us -> 1.57 us  [shards(): far = lax.ppermute(away_sent.astype(SENT), 'slab', beyond).astype(F32)]
  transfers between devices with their start and end apart: 7 -> 7, of which waited for: 6 -> 4; matrix products, arithmetic and copies ran while one was open for 0% -> 0% of each run, Pallas kernels for 1% -> 1%
where the time goes in v3:
time: 39.9 us; the launch traced here: 39.7 us
  starting transfers between devices  14.1 us (35%)
  blocking collectives  12.4 us (31%)
  waiting for transfers between devices  8.04 us (20%)
  Pallas kernels  3.68 us (9%)
  between operations  1.41 us (4%)
    all_to_all x1, blocking collectives, shards(): sums = lax.all_to_all(sums, ('harm', 'slab'), 0, 0, tiled=True)  12.4 us
    ppermute x1, starting transfers between devices, shards(): inner = lax.ppermute(held, 'slab', swap)  6.15 us
    ppermute x3, waiting for transfers between devices, shards(): lax.ppermute(message, 'harm', [(i, step(i, j, harmonics)) for i in range(...  5.04 us
    ppermute x3, starting transfers between devices, shards(): lax.ppermute(message, 'harm', [(i, step(i, j, harmonics)) for i in range(...  4.57 us
    pallas_call x7, Pallas kernels, call(): pl.pallas_call(body, out_shape=out_shape, in_specs=specs, out_specs=out_s...  3.68 us
    ppermute x1, starting transfers between devices, shards(): far = lax.ppermute(away_sent.astype(SENT), 'slab', beyond).astype(F32)  2.63 us
    ppermute x1, waiting for transfers between devices, shards(): far = lax.ppermute(away_sent.astype(SENT), 'slab', beyond).astype(F32)  1.57 us
    ppermute x1, waiting for transfers between devices, shards(): theirs = lax.ppermute(mine, 'slab', swap)  1.43 us
  transfers between devices with their start and end apart: 7, of which 4 were waited for; matrix products, arithmetic and copies ran while one was open for 0% of the time, Pallas kernels for 1%

profile of v3, /device:TPU:0, one launch (start us, length us, event | category | flops | bytes accessed | tf_op | source)
XLA Modules:
  0.0 39.7 jit_solution(11838780960132506564)
XLA Ops:
  0.6 1.1 %shard_map.59 = (f32[3,1,4,2,32,128]{5,4,3,2,1,0:T(8,128)S(1)}, f32[4,2,32,128]{3,2,1,0:T(8,128)S(1)}, f32[7,2,32,128]{3,2,1,0:T(8,128)S(1)}, f32[3,128]{1,0:T(4,128)S(1)}) custom-call(f32[3,1,4,2,32,128]{5,4,3,2,1,0:T(8,128)} %refs_0_.1, f32[3]{0:T(128)} %refs_1_.1, bf16[1,3,2,32,128]{4,3,2,1,0:T(8,128)(2,1)} %refs_2_.1), custom_call_target="tpu_custom_call" | custom-call | tf_op jit(solution)/shard_map/pallas_call | solution.py:24
  1.8 3.0 %collective-permute-start = (f16[7,2,32,128]{3,2,1,0:T(8,128)(2,1)S(1)}, f16[7,2,32,128]{3,2,1,0:T(8,128)(2,1)S(1)}, u32[]{:S(2)}, u32[]{:S(2)}) collective-permute-start(f16[7,2,32,128]{3,2,1,0:T(8,128)(2,1)S(1)} %convert_element_type.24), channel_id=1, source_target_pairs={{0,8},{8,0},{16,24},{24,16},{1,9},{9,1},{17,25},{25,17},{2,10},{10... | collective-permute-start | bytes 344072 | tf_op jit(solution)/shard_map/ppermute | solution.py:327
  4.8 1.5 %collective-permute-start.1 = (f16[7,2,32,128]{3,2,1,0:T(8,128)(2,1)S(1)}, f16[7,2,32,128]{3,2,1,0:T(8,128)(2,1)S(1)}, u32[]{:S(2)}, u32[]{:S(2)}) collective-permute-start(f16[7,2,32,128]{3,2,1,0:T(8,128)(2,1)S(1)} %convert_element_type.24), channel_id=1, source_target_pairs={{0,16},{8,24},{16,0},{24,8},{1,17},{9,25},{17,1},{25,9},{2,18},{10... | collective-permute-start | bytes 344072 | tf_op jit(solution)/shard_map/ppermute | solution.py:327
  6.4 0.0 collective-permute-start.2
  7.0 1.3 %collective-permute-done = f16[7,2,32,128]{3,2,1,0:T(8,128)(2,1)S(1)} collective-permute-done((f16[7,2,32,128]{3,2,1,0:T(8,128)(2,1)S(1)}, f16[7,2,32,128]{3,2,1,0:T(8,128)(2,1)S(1)}, u32[]{:S(2)}, u32[]{:S(2)}) %collective-permute-start) | collective-permute-done | bytes 114720 | tf_op jit(solution)/shard_map/ppermute | solution.py:327
  8.4 3.7 %collective-permute-done.1 = f16[7,2,32,128]{3,2,1,0:T(8,128)(2,1)S(1)} collective-permute-done((f16[7,2,32,128]{3,2,1,0:T(8,128)(2,1)S(1)}, f16[7,2,32,128]{3,2,1,0:T(8,128)(2,1)S(1)}, u32[]{:S(2)}, u32[]{:S(2)}) %collective-permute-start.1) | collective-permute-done | bytes 114720 | tf_op jit(solution)/shard_map/ppermute | solution.py:327
  12.1 0.0 collective-permute-done.2
  12.2 0.3 shard_map.61
  12.4 0.1 collective-permute-start.3
  12.5 1.4 %collective-permute-done.3.refs_1_.refs_5_ = f32[3,4,32,128]{3,2,1,0:T(8,128)S(1)} collective-permute-done((f32[3,4,32,128]{3,2,1,0:T(8,128)S(1)}, f32[3,4,32,128]{3,2,1,0:T(8,128)S(1)}, u32[]{:S(2)}, u32[]{:S(2)}) %collective-permute-start.3) | collective-permute-done | bytes 196640 | tf_op jit(solution)/shard_map/ppermute | solution.py:351
  14.0 0.7 %collective-permute-start.4 = (f16[5,4,32,128]{3,2,1,0:T(8,128)(2,1)S(1)}, f16[5,4,32,128]{3,2,1,0:T(8,128)(2,1)S(1)}, u32[]{:S(2)}, u32[]{:S(2)}) collective-permute-start(f16[5,4,32,128]{3,2,1,0:T(8,128)(2,1)S(1)} %convert_element_type.28), channel_id=1, source_target_pairs={{1,2},{3,4},{5,6},{2,1},{4,3},{6,5},{9,10},{11,12},{13,14},{10,9},... | collective-permute-start | bytes 491528 | tf_op jit(solution)/shard_map/ppermute | solution.py:363
  14.7 0.0 collective-permute-done.4
  14.8 6.2 %collective-permute-start.5 = (f32[3,4,32,128]{3,2,1,0:T(8,128)S(1)}, f32[3,4,32,128]{3,2,1,0:T(8,128)S(1)}, u32[]{:S(2)}, u32[]{:S(2)}) collective-permute-start(f32[3,4,32,128]{3,2,1,0:T(8,128)S(1)} %shard_map.63), channel_id=1, source_target_pairs={{0,1},{1,0},{2,3},{3,2},{4,5},{5,4},{6,7},{7,6},{8,9},{9,8},{10,11... | collective-permute-start | bytes 589832 | tf_op jit(solution)/shard_map/ppermute | solution.py:379
  20.9 2.6 %collective-permute-start.6 = (f16[4,32,128]{2,1,0:T(8,128)(2,1)S(1)}, f16[4,32,128]{2,1,0:T(8,128)(2,1)S(1)}, u32[]{:S(2)}, u32[]{:S(2)}) collective-permute-start(f16[4,32,128]{2,1,0:T(8,128)(2,1)S(1)} %convert_element_type.30), channel_id=1, source_target_pairs={{0,5},{1,4},{2,7},{3,6},{4,1},{5,0},{6,3},{7,2},{8,13},{9,12},{10,... | collective-permute-start | bytes 98312 | tf_op jit(solution)/shard_map/ppermute | solution.py:367
  23.6 0.2 shard_map.60.refs_1_
  23.8 1.6 %collective-permute-done.6 = f16[4,32,128]{2,1,0:T(8,128)(2,1)S(1)} collective-permute-done((f16[4,32,128]{2,1,0:T(8,128)(2,1)S(1)}, f16[4,32,128]{2,1,0:T(8,128)(2,1)S(1)}, u32[]{:S(2)}, u32[]{:S(2)}) %collective-permute-start.6) | collective-permute-done | bytes 32800 | tf_op jit(solution)/shard_map/ppermute | solution.py:367
  25.4 0.0 collective-permute-done.5.refs_8_
  25.4 1.2 %shard_map.64 = (f32[4,2,32,128]{3,2,1,0:T(8,128)S(1)}, f32[32,1,128]{2,1,0:T(1,128)S(1)}) custom-call(f32[1,128]{1,0:T(1,128)S(1)} %broadcast_in_dim.9.refs_0_, f32[1,128]{1,0:T(1,128)S(1)} %shard_map.60.refs_1_, f32[3,1,4,2,32,128]{5,4,3,2,1,0:T(8,128)S(1)} %get-tuple-element.12.basis.refs_2_.refs_1_, ...), custom_call_target="tpu_custom_call" | custom-call | tf_op jit(solution)/shard_map/pallas_call | solution.py:24
  26.5 12.4 %all_to_all.5.refs_3_ = f32[32,1,128]{2,1,0:T(1,128)S(1)} all-to-all(f32[32,1,128]{2,1,0:T(1,128)S(1)} %get-tuple-element.19), channel_id=1, replica_groups=mesh['harm'=4,'slab'=8] {'harm','slab'}, dimensions={0} | all-to-all | bytes 32768 | tf_op jit(solution)/shard_map/all_to_all | solution.py:392
  38.9 0.8 %shard_map.65 = (f32[1,4,2,32,128]{4,3,2,1,0:T(8,128)}, f32[4]{0:T(128)}) custom-call(f32[3,128]{1,0:T(4,128)S(1)} %get-tuple-element.11.refs_0_, f32[3,1,4,2,32,128]{5,4,3,2,1,0:T(8,128)S(1)} %get-tuple-element.12.basis.refs_2_.refs_1_, f32[4,2,32,128]{3,2,1,0:T(8,128)S(1)} %get-tuple-element.18.refs_2_, f32[32,1,128]{2,1,0:T(1,128)S(1)} %all_to_all.5.refs_3_), custom_call_target="tpu_custom_call" | custom-call | tf_op jit(solution)/shard_map/pallas_call | solution.py:24
  (11 shorter events, 0.2 us)
Async XLA Ops:
  1.8 6.6 %collective-permute-start = (f16[7,2,32,128]{3,2,1,0:T(8,128)(2,1)S(1)}, f16[7,2,32,128]{3,2,1,0:T(8,128)(2,1)S(1)}, u32[]{:S(2)}, u32[]{:S(2)}) collective-permute-start(f16[7,2,32,128]{3,2,1,0:T(8,128)(2,1)S(1)} %convert_element_type.24), channel_id=1, source_target_pairs={{0,8},{8,0},{16,24},{24,16},{1,9},{9,1},{17,25},{25,17},{2,10},{10... | collective-permute-start | bytes 344072 | tf_op jit(solution)/shard_map/ppermute | solution.py:327
  4.8 7.2 %collective-permute-start.1 = (f16[7,2,32,128]{3,2,1,0:T(8,128)(2,1)S(1)}, f16[7,2,32,128]{3,2,1,0:T(8,128)(2,1)S(1)}, u32[]{:S(2)}, u32[]{:S(2)}) collective-permute-start(f16[7,2,32,128]{3,2,1,0:T(8,128)(2,1)S(1)} %convert_element_type.24), channel_id=1, source_target_pairs={{0,16},{8,24},{16,0},{24,8},{1,17},{9,25},{17,1},{25,9},{2,18},{10... | collective-permute-start | bytes 344072 | tf_op jit(solution)/shard_map/ppermute | solution.py:327
  6.4 5.8 %collective-permute-start.2 = (f16[7,2,32,128]{3,2,1,0:T(8,128)(2,1)S(1)}, f16[7,2,32,128]{3,2,1,0:T(8,128)(2,1)S(1)}, u32[]{:S(2)}, u32[]{:S(2)}) collective-permute-start(f16[7,2,32,128]{3,2,1,0:T(8,128)(2,1)S(1)} %convert_element_type.24), channel_id=1, source_target_pairs={{0,24},{8,16},{16,8},{24,0},{1,25},{9,17},{17,9},{25,1},{2,26},{10... | collective-permute-start | bytes 344072 | tf_op jit(solution)/shard_map/ppermute | solution.py:327
  12.4 1.5 %collective-permute-start.3 = (f32[3,4,32,128]{3,2,1,0:T(8,128)S(1)}, f32[3,4,32,128]{3,2,1,0:T(8,128)S(1)}, u32[]{:S(2)}, u32[]{:S(2)}) collective-permute-start(f32[3,4,32,128]{3,2,1,0:T(8,128)S(1)} %get-tuple-element.15.refs_0_.refs_4_), channel_id=1, source_target_pairs={{0,1},{1,0},{2,3},{3,2},{4,5},{5,4},{6,7},{7,6},{8,9},{9,8},{10,11... | collective-permute-start | bytes 589832 | tf_op jit(solution)/shard_map/ppermute | solution.py:351
  14.0 0.7 %collective-permute-start.4 = (f16[5,4,32,128]{3,2,1,0:T(8,128)(2,1)S(1)}, f16[5,4,32,128]{3,2,1,0:T(8,128)(2,1)S(1)}, u32[]{:S(2)}, u32[]{:S(2)}) collective-permute-start(f16[5,4,32,128]{3,2,1,0:T(8,128)(2,1)S(1)} %convert_element_type.28), channel_id=1, source_target_pairs={{1,2},{3,4},{5,6},{2,1},{4,3},{6,5},{9,10},{11,12},{13,14},{10,9},... | collective-permute-start | bytes 491528 | tf_op jit(solution)/shard_map/ppermute | solution.py:363
  14.8 10.6 %collective-permute-start.5 = (f32[3,4,32,128]{3,2,1,0:T(8,128)S(1)}, f32[3,4,32,128]{3,2,1,0:T(8,128)S(1)}, u32[]{:S(2)}, u32[]{:S(2)}) collective-permute-start(f32[3,4,32,128]{3,2,1,0:T(8,128)S(1)} %shard_map.63), channel_id=1, source_target_pairs={{0,1},{1,0},{2,3},{3,2},{4,5},{5,4},{6,7},{7,6},{8,9},{9,8},{10,11... | collective-permute-start | bytes 589832 | tf_op jit(solution)/shard_map/ppermute | solution.py:379
  20.9 4.4 %collective-permute-start.6 = (f16[4,32,128]{2,1,0:T(8,128)(2,1)S(1)}, f16[4,32,128]{2,1,0:T(8,128)(2,1)S(1)}, u32[]{:S(2)}, u32[]{:S(2)}) collective-permute-start(f16[4,32,128]{2,1,0:T(8,128)(2,1)S(1)} %convert_element_type.30), channel_id=1, source_target_pairs={{0,5},{1,4},{2,7},{3,6},{4,1},{5,0},{6,3},{7,2},{8,13},{9,12},{10,... | collective-permute-start | bytes 98312 | tf_op jit(solution)/shard_map/ppermute | solution.py:367

commit v4 on v3

--- a/solution.py
+++ b/solution.py
@@ -156,92 +156,121 @@
     message[2 * planes] = away[...] * rescale
 
 
-def inner_kernel(mine, theirs, away, outer, message, *, unscale):
-    planes = mine.shape[0] - 1
+def inner_kernel(away, outer, message, *, unscale):
+    planes = message.shape[0] - 1
     message[0] = outer[0] * unscale + away[...]
     for t in range(1, planes):
         message[t] = outer[t] * unscale
-    own = mine[0] + outer[2 * planes] * unscale
-    if planes == 1:
-        own = own + theirs[planes]
-    message[planes] = own
-
-
-def chebyshev_kernel(shift, gram, basis, vec, mine, theirs, away, outer, inner, far, change, sums, *, unscale):
-    count, fields = basis.shape[0], vec.shape[0]
-    planes = mine.shape[0] - 1
+    message[planes] = outer[2 * planes] * unscale
+
+
+def neighbours():
     slab, slabs = lax.axis_index("slab"), lax.axis_size("slab")
-    core = parity()
-    flip = core == 1
+    flip = parity() == 1
     chip, chips = lax.div(slab, 2), slabs // 2
-    has_low = (chip > 0).astype(F32)
-    has_high = (chip < chips - 1).astype(F32)
-    has_outer = jnp.where(flip, has_high, has_low)
-    has_inner = jnp.where(flip, has_low, has_high)
-    two_away = jnp.where(flip, chips - 1 - chip, chip) > 1
-    has_far = two_away.astype(F32)
-    own_shift = shift[...]
-    middle = own_shift + 6.0 * VISCOSITY
+    before = jnp.where(flip, chips - 1 - chip, chip)
+    after = jnp.where(flip, chip, chips - 1 - chip)
+    return [x.astype(F32) for x in (before > 0, after > 0, before > 1)]
+
+
+def recurrence(shift):
+    middle = shift + 6.0 * VISCOSITY
     half_span = 6.0 * VISCOSITY
     span_ratio = middle / half_span
-    ratio = 1.0 / span_ratio
-    gains, far_gain = [], 1.0 / middle
+    first = 1.0 / middle
+    ratio, unit = 1.0 / span_ratio, 1.0
+    units, same, past = [], [], []
+    kept = gained = None
     for _ in range(SWEEPS):
         following = 1.0 / (2.0 * span_ratio - ratio)
-        gains.append((following * ratio, 2.0 * following / half_span))
-        far_gain = far_gain * (gains[-1][1] * VISCOSITY)
-        ratio = following
-    depth = SWEEPS
-    first = 1.0 / middle
+        gain = 2.0 * following / half_span * VISCOSITY
+        inverse = 1.0 / gain
+        keep = following * ratio * inverse
+        if gained is None:
+            same.append(keep)
+            past.append(None)
+        else:
+            same.append(keep + gained - middle * (1.0 / VISCOSITY))
+            past.append(kept * gained)
+        unit = unit * gain
+        units.append(unit)
+        kept, gained, ratio = keep, inverse, following
+    return first, units, same, past
+
+
+def sweeps(applied, outside, planes, coefficients):
+    first, units, same, past = coefficients
+    direction = {p: v * first if p not in outside else v * (first * outside[p]) for p, v in applied.items()}
+    solution = {t: direction[t] for t in range(planes) if t in direction}
+    previous = {}
+    for n in range(SWEEPS):
+        reach = SWEEPS - 1 - n
+        fresh = {}
+        for p in range(-reach, planes + reach):
+            terms = [direction[q] for q in (p - 1, p + 1) if q in direction]
+            if p in direction:
+                d = direction[p]
+                terms += [y_up(d), y_down(d), z_up(d), z_down(d), same[n] * d]
+            if not terms:
+                continue
+            value = terms[0]
+            for term in terms[1:]:
+                value = value + term
+            if p in previous:
+                value = value - past[n] * previous[p]
+            fresh[p] = value if p not in outside else outside[p] * value
+        previous, direction = direction, fresh
+        for t in range(planes):
+            if t in direction:
+                part = units[n] * direction[t]
+                solution[t] = solution[t] + part if t in solution else part
+    return solution
+
+
+def near_kernel(shift, mine, theirs, away, outer, part, *, unscale):
+    fields, planes = part.shape[1], part.shape[0]
+    has_outer, has_inner, _ = neighbours()
+    coefficients = recurrence(shift[...])
+    for f in range(fields):
+        applied, outside = {}, {2 * planes + t: has_inner for t in range(planes)}
+        for i in range(2 * planes):
+            value = outer[i, f] * unscale
+            applied[-1 - i] = value + away[f] if i == 0 else value
+            outside[-1 - i] = has_outer
+        for t in range(planes):
+            own, other = mine[t, f], theirs[t, f]
+            if t == planes - 1:
+                own, other = own + theirs[planes, f], other + mine[planes, f]
+            if t == 0:
+                own = own + outer[2 * planes, f] * unscale
+            applied[t] = own
+            applied[2 * planes - 1 - t] = other
+        solution = sweeps(applied, outside, planes, coefficients)
+        for t in range(planes):
+            part[t, f] = solution[t]
+
+
+def chebyshev_kernel(shift, gram, basis, vec, part, inner, far, change, sums, *, unscale):
+    count, fields = basis.shape[0], vec.shape[0]
+    planes = part.shape[0]
+    _, has_inner, has_far = neighbours()
+    flip = parity() == 1
+    coefficients = recurrence(shift[...])
+    far_gain = coefficients[0] * coefficients[1][-1] * (unscale * has_far)
     totals = [None] * (1 + count)
     for f in range(fields):
-        remainder = [outer[depth - 1 - i, f] * unscale for i in range(depth - 1)]
-        remainder.append(outer[0, f] * unscale + away[f])
-        scale = [has_outer] * depth + [None] * (2 * planes) + [has_inner] * planes
-        for t in range(planes):
-            value = mine[t, f]
-            if t == planes - 1:
-                value = value + theirs[planes, f]
+        applied = {2 * planes - 1: inner[planes, f]}
+        outside = {}
+        for t in range(planes):
+            applied[2 * planes + t] = inner[t, f]
+            outside[2 * planes + t] = has_inner
+        solution = sweeps(applied, outside, planes, coefficients)
+        for t in range(planes):
+            x = jnp.where(flip, planes - 1 - t, t)
+            value = part[t, f] + solution[t]
             if t == 0:
-                value = value + outer[2 * planes, f] * unscale
-            remainder.append(value)
-        for t in range(planes - 1, -1, -1):
-            if t == 0:
-                remainder.append(inner[planes, f])
-            elif t == planes - 1:
-                remainder.append(theirs[t, f] + mine[planes, f])
-            else:
-                remainder.append(theirs[t, f])
-        for t in range(planes):
-            remainder.append(inner[t, f])
-        direction = [
-            (r * first) if m is None else (r * (first * m)) for r, m in zip(remainder, scale)
-        ]
-        solution = [direction[depth + t] for t in range(planes)]
-        low = 0
-        for sweep in range(SWEEPS):
-            keep, gain = gains[sweep]
-            nothing = low + 1
-            end = low + len(direction) - 1
-            next_remainder, next_direction = [], []
-            for position in range(nothing, end):
-                i = position - low
-                d = direction[i]
-                around = direction[i + 1] + direction[i - 1] + y_up(d) + y_down(d) + z_up(d) + z_down(d)
-                r = remainder[i] - (middle * d - VISCOSITY * around)
-                m = scale[position]
-                if m is None:
-                    n = keep * d + gain * r
-                else:
-                    n = (keep * m) * d + (gain * m) * r
-                next_remainder.append(r)
-                next_direction.append(n)
-            remainder, direction, low = next_remainder, next_direction, low + 1
-            solution = [s + direction[depth - low + t] for t, s in enumerate(solution)]
-        solution[0] = solution[0] + (far_gain * unscale * has_far) * far[f]
-        for t in range(planes):
-            x = jnp.where(flip, planes - 1 - t, t)
-            moved = solution[t] - vec[f, x]
+                value = value + far_gain * far[f]
+            moved = value - vec[f, x]
             change[f, x] = moved
             parts = [moved * moved] + [basis[j, 0, f, x] * moved for j in range(count)]
             totals = [p if q is None else q + p for q, p in zip(totals, parts)]
@@ -372,12 +401,23 @@
     held = call(
         inner_body,
         jax.ShapeDtypeStruct((planes + 1, fields, ny, nz), F32),
-        (mine, theirs, away, outer),
-        [VMEM] * 4,
+        (away, outer),
+        [VMEM] * 2,
         VMEM,
     )
     inner = lax.ppermute(held, "slab", swap)
     devices = harmonics * slabs
+
+    def near_body(*refs):
+        near_kernel(*refs, unscale=1.0 / applied_scale)
+
+    part = call(
+        near_body,
+        jax.ShapeDtypeStruct((planes, fields, ny, nz), F32),
+        (shift, mine, theirs, away, outer),
+        [VMEM] * 5,
+        VMEM,
+    )
 
     def chebyshev_body(*refs):
         chebyshev_kernel(*refs, unscale=1.0 / applied_scale)
@@ -385,8 +425,8 @@
     change, sums = call(
         chebyshev_body,
         [jax.ShapeDtypeStruct(shape, F32), jax.ShapeDtypeStruct((devices, 1, nz), F32)],
-        (shift, gram, basis, vec, mine, theirs, away, outer, inner, far),
-        [VMEM] * 10,
+        (shift, gram, basis, vec, part, inner, far),
+        [VMEM] * 7,
         [VMEM, VMEM],
     )
     sums = lax.all_to_all(sums, ("harm", "slab"), 0, 0, tiled=True)

time: 39.9 us -> 40.2 us (level)
  waiting for transfers between devices: 8.04 us -> 7.52 us
    ppermute x3, waiting for transfers between devices: 5.04 us -> 4.51 us  [shards(): lax.ppermute(message, 'harm', [(i, step(i, j, harmonics)) for i in range(...]
    pallas_call x7 -> x8, Pallas kernels: 3.68 us -> 4.04 us  [call(): pl.pallas_call(body, out_shape=out_shape, in_specs=specs, out_specs=out_s...]
  transfers between devices with their start and end apart: 7 -> 7, of which waited for: 4 -> 5; matrix products, arithmetic and copies ran while one was open for 0% -> 0% of each run, Pallas kernels for 1% -> 3%
where the time goes in v4:
time: 40.2 us; the launch traced here: 40 us
  starting transfers between devices  14.2 us (35%)
  blocking collectives  12.7 us (32%)
  waiting for transfers between devices  7.52 us (19%)
  Pallas kernels  4.04 us (10%)
  between operations  1.42 us (4%)
    all_to_all x1, blocking collectives, shards(): sums = lax.all_to_all(sums, ('harm', 'slab'), 0, 0, tiled=True)  12.7 us
    ppermute x1, starting transfers between devices, shards(): inner = lax.ppermute(held, 'slab', swap)  6.15 us
    ppermute x3, starting transfers between devices, shards(): lax.ppermute(message, 'harm', [(i, step(i, j, harmonics)) for i in range(...  4.63 us
    ppermute x3, waiting for transfers between devices, shards(): lax.ppermute(message, 'harm', [(i, step(i, j, harmonics)) for i in range(...  4.51 us
    pallas_call x8, Pallas kernels, call(): pl.pallas_call(body, out_shape=out_shape, in_specs=specs, out_specs=out_s...  4.04 us
    ppermute x1, starting transfers between devices, shards(): far = lax.ppermute(away_sent.astype(SENT), 'slab', beyond).astype(F32)  2.63 us
    ppermute x1, waiting for transfers between devices, shards(): far = lax.ppermute(away_sent.astype(SENT), 'slab', beyond).astype(F32)  1.57 us
    ppermute x1, waiting for transfers between devices, shards(): theirs = lax.ppermute(mine, 'slab', swap)  1.43 us
  transfers between devices with their start and end apart: 7, of which 5 were waited for; matrix products, arithmetic and copies ran while one was open for 0% of the time, Pallas kernels for 3%

profile of v4, /device:TPU:0, one launch (start us, length us, event | category | flops | bytes accessed | tf_op | source)
XLA Modules:
  0.0 40.0 jit_solution(11694367922710134597)
XLA Ops:
  0.6 1.1 %shard_map.59 = (f32[3,1,4,2,32,128]{5,4,3,2,1,0:T(8,128)S(1)}, f32[4,2,32,128]{3,2,1,0:T(8,128)S(1)}, f32[7,2,32,128]{3,2,1,0:T(8,128)S(1)}, f32[3,128]{1,0:T(4,128)S(1)}) custom-call(f32[3,1,4,2,32,128]{5,4,3,2,1,0:T(8,128)} %refs_0_.1, f32[3]{0:T(128)} %refs_1_.1, bf16[1,3,2,32,128]{4,3,2,1,0:T(8,128)(2,1)} %refs_2_.1), custom_call_target="tpu_custom_call" | custom-call | tf_op jit(solution)/shard_map/pallas_call | solution.py:24
  1.8 4.0 %collective-permute-start.2 = (f16[7,2,32,128]{3,2,1,0:T(8,128)(2,1)S(1)}, f16[7,2,32,128]{3,2,1,0:T(8,128)(2,1)S(1)}, u32[]{:S(2)}, u32[]{:S(2)}) collective-permute-start(f16[7,2,32,128]{3,2,1,0:T(8,128)(2,1)S(1)} %convert_element_type.24), channel_id=1, source_target_pairs={{0,24},{8,16},{16,8},{24,0},{1,25},{9,17},{17,9},{25,1},{2,26},{10... | collective-permute-start | bytes 344072 | tf_op jit(solution)/shard_map/ppermute | solution.py:356
  5.8 0.5 %collective-permute-start.1 = (f16[7,2,32,128]{3,2,1,0:T(8,128)(2,1)S(1)}, f16[7,2,32,128]{3,2,1,0:T(8,128)(2,1)S(1)}, u32[]{:S(2)}, u32[]{:S(2)}) collective-permute-start(f16[7,2,32,128]{3,2,1,0:T(8,128)(2,1)S(1)} %convert_element_type.24), channel_id=1, source_target_pairs={{0,16},{8,24},{16,0},{24,8},{1,17},{9,25},{17,1},{25,9},{2,18},{10... | collective-permute-start | bytes 344072 | tf_op jit(solution)/shard_map/ppermute | solution.py:356
  6.3 0.1 collective-permute-start
  7.1 2.2 %collective-permute-done.2 = f16[7,2,32,128]{3,2,1,0:T(8,128)(2,1)S(1)} collective-permute-done((f16[7,2,32,128]{3,2,1,0:T(8,128)(2,1)S(1)}, f16[7,2,32,128]{3,2,1,0:T(8,128)(2,1)S(1)}, u32[]{:S(2)}, u32[]{:S(2)}) %collective-permute-start.2) | collective-permute-done | bytes 114720 | tf_op jit(solution)/shard_map/ppermute | solution.py:356
  9.4 2.0 %collective-permute-done.1 = f16[7,2,32,128]{3,2,1,0:T(8,128)(2,1)S(1)} collective-permute-done((f16[7,2,32,128]{3,2,1,0:T(8,128)(2,1)S(1)}, f16[7,2,32,128]{3,2,1,0:T(8,128)(2,1)S(1)}, u32[]{:S(2)}, u32[]{:S(2)}) %collective-permute-start.1) | collective-permute-done | bytes 114720 | tf_op jit(solution)/shard_map/ppermute | solution.py:356
  11.4 0.2 collective-permute-done
  11.7 0.3 shard_map.61
  12.0 0.1 collective-permute-start.3
  12.0 1.4 %collective-permute-done.3.refs_1_.refs_2_ = f32[3,4,32,128]{3,2,1,0:T(8,128)S(1)} collective-permute-done((f32[3,4,32,128]{3,2,1,0:T(8,128)S(1)}, f32[3,4,32,128]{3,2,1,0:T(8,128)S(1)}, u32[]{:S(2)}, u32[]{:S(2)}) %collective-permute-start.3) | collective-permute-done | bytes 196640 | tf_op jit(solution)/shard_map/ppermute | solution.py:380
  13.5 0.7 %collective-permute-start.4 = (f16[5,4,32,128]{3,2,1,0:T(8,128)(2,1)S(1)}, f16[5,4,32,128]{3,2,1,0:T(8,128)(2,1)S(1)}, u32[]{:S(2)}, u32[]{:S(2)}) collective-permute-start(f16[5,4,32,128]{3,2,1,0:T(8,128)(2,1)S(1)} %convert_element_type.28), channel_id=1, source_target_pairs={{1,2},{3,4},{5,6},{2,1},{4,3},{6,5},{9,10},{11,12},{13,14},{10,9},... | collective-permute-start | bytes 491528 | tf_op jit(solution)/shard_map/ppermute | solution.py:392
  14.2 0.0 collective-permute-done.4
  14.3 6.2 %collective-permute-start.5 = (f32[3,4,32,128]{3,2,1,0:T(8,128)S(1)}, f32[3,4,32,128]{3,2,1,0:T(8,128)S(1)}, u32[]{:S(2)}, u32[]{:S(2)}) collective-permute-start(f32[3,4,32,128]{3,2,1,0:T(8,128)S(1)} %shard_map.64), channel_id=1, source_target_pairs={{0,1},{1,0},{2,3},{3,2},{4,5},{5,4},{6,7},{7,6},{8,9},{9,8},{10,11... | collective-permute-start | bytes 589832 | tf_op jit(solution)/shard_map/ppermute | solution.py:408
  20.5 2.6 %collective-permute-start.6 = (f16[4,32,128]{2,1,0:T(8,128)(2,1)S(1)}, f16[4,32,128]{2,1,0:T(8,128)(2,1)S(1)}, u32[]{:S(2)}, u32[]{:S(2)}) collective-permute-start(f16[4,32,128]{2,1,0:T(8,128)(2,1)S(1)} %convert_element_type.30), channel_id=1, source_target_pairs={{0,5},{1,4},{2,7},{3,6},{4,1},{5,0},{6,3},{7,2},{8,13},{9,12},{10,... | collective-permute-start | bytes 98312 | tf_op jit(solution)/shard_map/ppermute | solution.py:396
  23.1 0.2 shard_map.60.refs_1_
  23.3 1.6 %collective-permute-done.6 = f16[4,32,128]{2,1,0:T(8,128)(2,1)S(1)} collective-permute-done((f16[4,32,128]{2,1,0:T(8,128)(2,1)S(1)}, f16[4,32,128]{2,1,0:T(8,128)(2,1)S(1)}, u32[]{:S(2)}, u32[]{:S(2)}) %collective-permute-start.6) | collective-permute-done | bytes 32800 | tf_op jit(solution)/shard_map/ppermute | solution.py:396
  24.9 1.1 %shard_map.63.refs_4_ = f32[2,4,32,128]{3,2,1,0:T(8,128)S(1)} custom-call(f32[1,128]{1,0:T(1,128)S(1)} %broadcast_in_dim.9.refs_0_, f32[3,4,32,128]{3,2,1,0:T(8,128)S(1)} %get-tuple-element.15.refs_0_.refs_1_, f32[3,4,32,128]{3,2,1,0:T(8,128)S(1)} %collective-permute-done.3.refs_1_.refs_2_, f32[4,32,128]{2,1,0:T(8,128)S(1)} %get-tuple-element.16.refs_2_.refs_3_.refs_0_, ...), custom_call_target="tpu_custom_call" | custom-call | tf_op jit(solution)/shard_map/pallas_call | solution.py:24
  26.0 0.0 collective-permute-done.5.refs_5_
  26.0 0.4 %shard_map.65 = (f32[4,2,32,128]{3,2,1,0:T(8,128)S(1)}, f32[32,1,128]{2,1,0:T(1,128)S(1)}) custom-call(f32[1,128]{1,0:T(1,128)S(1)} %broadcast_in_dim.9.refs_0_, f32[1,128]{1,0:T(1,128)S(1)} %shard_map.60.refs_1_, f32[3,1,4,2,32,128]{5,4,3,2,1,0:T(8,128)S(1)} %get-tuple-element.12.basis.refs_2_.refs_1_, ...), custom_call_target="tpu_custom_call" | custom-call | tf_op jit(solution)/shard_map/pallas_call | solution.py:24
  26.4 12.7 %all_to_all.5.refs_3_ = f32[32,1,128]{2,1,0:T(1,128)S(1)} all-to-all(f32[32,1,128]{2,1,0:T(1,128)S(1)} %get-tuple-element.19), channel_id=1, replica_groups=mesh['harm'=4,'slab'=8] {'harm','slab'}, dimensions={0} | all-to-all | bytes 32768 | tf_op jit(solution)/shard_map/all_to_all | solution.py:432
  39.2 0.8 %shard_map.66 = (f32[1,4,2,32,128]{4,3,2,1,0:T(8,128)}, f32[4]{0:T(128)}) custom-call(f32[3,128]{1,0:T(4,128)S(1)} %get-tuple-element.11.refs_0_, f32[3,1,4,2,32,128]{5,4,3,2,1,0:T(8,128)S(1)} %get-tuple-element.12.basis.refs_2_.refs_1_, f32[4,2,32,128]{3,2,1,0:T(8,128)S(1)} %get-tuple-element.18.refs_2_, f32[32,1,128]{2,1,0:T(1,128)S(1)} %all_to_all.5.refs_3_), custom_call_target="tpu_custom_call" | custom-call | tf_op jit(solution)/shard_map/pallas_call | solution.py:24
  (11 shorter events, 0.2 us)
Async XLA Ops:
  1.8 7.5 %collective-permute-start.2 = (f16[7,2,32,128]{3,2,1,0:T(8,128)(2,1)S(1)}, f16[7,2,32,128]{3,2,1,0:T(8,128)(2,1)S(1)}, u32[]{:S(2)}, u32[]{:S(2)}) collective-permute-start(f16[7,2,32,128]{3,2,1,0:T(8,128)(2,1)S(1)} %convert_element_type.24), channel_id=1, source_target_pairs={{0,24},{8,16},{16,8},{24,0},{1,25},{9,17},{17,9},{25,1},{2,26},{10... | collective-permute-start | bytes 344072 | tf_op jit(solution)/shard_map/ppermute | solution.py:356
  5.8 5.6 %collective-permute-start.1 = (f16[7,2,32,128]{3,2,1,0:T(8,128)(2,1)S(1)}, f16[7,2,32,128]{3,2,1,0:T(8,128)(2,1)S(1)}, u32[]{:S(2)}, u32[]{:S(2)}) collective-permute-start(f16[7,2,32,128]{3,2,1,0:T(8,128)(2,1)S(1)} %convert_element_type.24), channel_id=1, source_target_pairs={{0,16},{8,24},{16,0},{24,8},{1,17},{9,25},{17,1},{25,9},{2,18},{10... | collective-permute-start | bytes 344072 | tf_op jit(solution)/shard_map/ppermute | solution.py:356
  6.3 5.3 %collective-permute-start = (f16[7,2,32,128]{3,2,1,0:T(8,128)(2,1)S(1)}, f16[7,2,32,128]{3,2,1,0:T(8,128)(2,1)S(1)}, u32[]{:S(2)}, u32[]{:S(2)}) collective-permute-start(f16[7,2,32,128]{3,2,1,0:T(8,128)(2,1)S(1)} %convert_element_type.24), channel_id=1, source_target_pairs={{0,8},{8,0},{16,24},{24,16},{1,9},{9,1},{17,25},{25,17},{2,10},{10... | collective-permute-start | bytes 344072 | tf_op jit(solution)/shard_map/ppermute | solution.py:356
  12.0 1.5 %collective-permute-start.3 = (f32[3,4,32,128]{3,2,1,0:T(8,128)S(1)}, f32[3,4,32,128]{3,2,1,0:T(8,128)S(1)}, u32[]{:S(2)}, u32[]{:S(2)}) collective-permute-start(f32[3,4,32,128]{3,2,1,0:T(8,128)S(1)} %get-tuple-element.15.refs_0_.refs_1_), channel_id=1, source_target_pairs={{0,1},{1,0},{2,3},{3,2},{4,5},{5,4},{6,7},{7,6},{8,9},{9,8},{10,11... | collective-permute-start | bytes 589832 | tf_op jit(solution)/shard_map/ppermute | solution.py:380
  13.5 0.7 %collective-permute-start.4 = (f16[5,4,32,128]{3,2,1,0:T(8,128)(2,1)S(1)}, f16[5,4,32,128]{3,2,1,0:T(8,128)(2,1)S(1)}, u32[]{:S(2)}, u32[]{:S(2)}) collective-permute-start(f16[5,4,32,128]{3,2,1,0:T(8,128)(2,1)S(1)} %convert_element_type.28), channel_id=1, source_target_pairs={{1,2},{3,4},{5,6},{2,1},{4,3},{6,5},{9,10},{11,12},{13,14},{10,9},... | collective-permute-start | bytes 491528 | tf_op jit(solution)/shard_map/ppermute | solution.py:392
  14.3 11.7 %collective-permute-start.5 = (f32[3,4,32,128]{3,2,1,0:T(8,128)S(1)}, f32[3,4,32,128]{3,2,1,0:T(8,128)S(1)}, u32[]{:S(2)}, u32[]{:S(2)}) collective-permute-start(f32[3,4,32,128]{3,2,1,0:T(8,128)S(1)} %shard_map.64), channel_id=1, source_target_pairs={{0,1},{1,0},{2,3},{3,2},{4,5},{5,4},{6,7},{7,6},{8,9},{9,8},{10,11... | collective-permute-start | bytes 589832 | tf_op jit(solution)/shard_map/ppermute | solution.py:408
  20.5 4.4 %collective-permute-start.6 = (f16[4,32,128]{2,1,0:T(8,128)(2,1)S(1)}, f16[4,32,128]{2,1,0:T(8,128)(2,1)S(1)}, u32[]{:S(2)}, u32[]{:S(2)}) collective-permute-start(f16[4,32,128]{2,1,0:T(8,128)(2,1)S(1)} %convert_element_type.30), channel_id=1, source_target_pairs={{0,5},{1,4},{2,7},{3,6},{4,1},{5,0},{6,3},{7,2},{8,13},{9,12},{10,... | collective-permute-start | bytes 98312 | tf_op jit(solution)/shard_map/ppermute | solution.py:396

commit v5 on v4

--- a/solution.py
+++ b/solution.py
@@ -68,10 +68,10 @@
     vector = count * WEIGHT_MAX * BASIS_MAX
     flux = harmonics * FLOW_MAX * vector
     applied = (SHIFT_MAX + 12.0 * VISCOSITY) * vector + DIRS * flux
-    return [2.0 ** math.floor(math.log2(SENT_MAX / bound)) for bound in (vector, applied)]
-
-
-def start_kernel(basis_in, weights_in, flow_in, basis, vec, message, scalars, weights, flow, sems, *, rescale):
+    return [2.0 ** math.floor(math.log2(SENT_MAX / bound)) for bound in (vector, FLOW_MAX, applied)]
+
+
+def start_kernel(basis_in, weights_in, flow_in, basis, vec, message, scalars, weights, flow, sems, *, rescale, flow_rescale):
     count, fields = basis.shape[0], basis.shape[2]
     copies = [pltpu.make_async_copy(weights_in, weights, sems.at[0])]
     copies.append(pltpu.make_async_copy(flow_in, flow, sems.at[1]))
@@ -86,9 +86,13 @@
             total = total + weights[j] * basis[j, 0, f]
         vec[f] = total
         message[f] = total * rescale
-    message[fields:] = flow[0].astype(F32)
+    message[fields:] = flow[0].astype(F32) * flow_rescale
     for j in range(count):
         scalars[j : j + 1] = jnp.full((1, scalars.shape[1]), weights[j], F32)
+
+
+def whole_sum(plane):
+    return jnp.sum(jnp.sum(plane, axis=0, keepdims=True), axis=1, keepdims=True)
 
 
 def gram_kernel(basis, sums):
@@ -97,12 +101,12 @@
     line, place = jnp.zeros(sums.shape, F32), 1 + count
     for i in range(count):
         for j in range(i, count):
-            line = jnp.where(lanes == place, jnp.sum(basis[i, 0] * basis[j, 0]), line)
+            line = jnp.where(lanes == place, whole_sum(jnp.sum(basis[i, 0] * basis[j, 0], axis=(0, 1))), line)
             place += 1
     sums[...] = line
 
 
-def flux_kernel(shift, vec, *refs, harmonics, unscale, rescale):
+def flux_kernel(shift, vec, *refs, harmonics, unscale, flow_unscale, rescale):
     messages = refs[:harmonics]
     partial, away, away_sent, flows = refs[harmonics:]
     fields, planes = vec.shape[0], vec.shape[1]
@@ -118,9 +122,10 @@
         for t in range(planes):
             x = jnp.where(flip, planes - 1 - t, t)
             center = vec[f, x]
-            flux = [flows[0, d, x] * center for d in range(DIRS)]
+            scaled = center * flow_unscale
+            flux = [flows[0, d, x] * scaled for d in range(DIRS)]
             for j in range(1, harmonics):
-                other = messages[j][f, x] * unscale
+                other = messages[j][f, x] * (unscale * flow_unscale)
                 row = lax.rem(harm - step_back(harm, j, harmonics) + harmonics, harmonics)
                 flux = [flux[d] + flows[row, d, x] * other for d in range(DIRS)]
             half_y = 0.5 * flux[1]
@@ -278,7 +283,7 @@
     line = gram[...]
     place = 0
     for total in totals:
-        line = jnp.where(lanes == place, jnp.sum(total), line)
+        line = jnp.where(lanes == place, whole_sum(total), line)
         place += 1
     sums[...] = jnp.broadcast_to(line[None], sums.shape)
 
@@ -327,10 +332,10 @@
     harmonics, slabs = lax.axis_size("harm"), lax.axis_size("slab")
     assert 2 * planes == SWEEPS and slabs % 2 == 0
     shape = (fields, planes, ny, nz)
-    vec_scale, applied_scale = scales(count, harmonics)
+    vec_scale, flow_scale, applied_scale = scales(count, harmonics)
 
     def start_body(*refs):
-        start_kernel(*refs, rescale=vec_scale)
+        start_kernel(*refs, rescale=vec_scale, flow_rescale=flow_scale)
 
     basis, vec, message, scalars = call(
         start_body,
@@ -358,7 +363,7 @@
     ]
 
     def flux_body(*refs):
-        flux_kernel(*refs, harmonics=harmonics, unscale=1.0 / vec_scale, rescale=applied_scale)
+        flux_kernel(*refs, harmonics=harmonics, unscale=1.0 / vec_scale, flow_unscale=1.0 / flow_scale, rescale=applied_scale)
 
     mine, away, away_sent = call(
         flux_body,

time: 40.2 us -> 40.2 us (level)
  no operation moved by 1% of the time
where the time goes in v5:
time: 40.2 us; the launch traced here: 40 us
  starting transfers between devices  14.2 us (35%)
  blocking collectives  12.7 us (32%)
  waiting for transfers between devices  7.59 us (19%)
  Pallas kernels  3.96 us (10%)
  between operations  1.4 us (3%)
    all_to_all x1, blocking collectives, shards(): sums = lax.all_to_all(sums, ('harm', 'slab'), 0, 0, tiled=True)  12.7 us
    ppermute x1, starting transfers between devices, shards(): inner = lax.ppermute(held, 'slab', swap)  6.15 us
    ppermute x3, starting transfers between devices, shards(): lax.ppermute(message, 'harm', [(i, step(i, j, harmonics)) for i in range(...  4.63 us
    ppermute x3, waiting for transfers between devices, shards(): lax.ppermute(message, 'harm', [(i, step(i, j, harmonics)) for i in range(...  4.51 us
    pallas_call x8, Pallas kernels, call(): pl.pallas_call(body, out_shape=out_shape, in_specs=specs, out_specs=out_s...  3.96 us
    ppermute x1, starting transfers between devices, shards(): far = lax.ppermute(away_sent.astype(SENT), 'slab', beyond).astype(F32)  2.63 us
    ppermute x1, waiting for transfers between devices, shards(): far = lax.ppermute(away_sent.astype(SENT), 'slab', beyond).astype(F32)  1.64 us
    ppermute x1, waiting for transfers between devices, shards(): theirs = lax.ppermute(mine, 'slab', swap)  1.43 us
  transfers between devices with their start and end apart: 7, of which 5 were waited for; matrix products, arithmetic and copies ran while one was open for 0% of the time, Pallas kernels for 3%

profile of v5, /device:TPU:0, one launch (start us, length us, event | category | flops | bytes accessed | tf_op | source)
XLA Modules:
  0.0 40.0 jit_solution(7922200377662509338)
XLA Ops:
  0.6 1.1 %shard_map.59 = (f32[3,1,4,2,32,128]{5,4,3,2,1,0:T(8,128)S(1)}, f32[4,2,32,128]{3,2,1,0:T(8,128)S(1)}, f32[7,2,32,128]{3,2,1,0:T(8,128)S(1)}, f32[3,128]{1,0:T(4,128)S(1)}) custom-call(f32[3,1,4,2,32,128]{5,4,3,2,1,0:T(8,128)} %refs_0_.1, f32[3]{0:T(128)} %refs_1_.1, bf16[1,3,2,32,128]{4,3,2,1,0:T(8,128)(2,1)} %refs_2_.1), custom_call_target="tpu_custom_call" | custom-call | tf_op jit(solution)/shard_map/pallas_call | solution.py:24
  1.8 4.0 %collective-permute-start.2 = (f16[7,2,32,128]{3,2,1,0:T(8,128)(2,1)S(1)}, f16[7,2,32,128]{3,2,1,0:T(8,128)(2,1)S(1)}, u32[]{:S(2)}, u32[]{:S(2)}) collective-permute-start(f16[7,2,32,128]{3,2,1,0:T(8,128)(2,1)S(1)} %convert_element_type.24), channel_id=1, source_target_pairs={{0,24},{8,16},{16,8},{24,0},{1,25},{9,17},{17,9},{25,1},{2,26},{10... | collective-permute-start | bytes 344072 | tf_op jit(solution)/shard_map/ppermute | solution.py:361
  5.8 0.5 %collective-permute-start.1 = (f16[7,2,32,128]{3,2,1,0:T(8,128)(2,1)S(1)}, f16[7,2,32,128]{3,2,1,0:T(8,128)(2,1)S(1)}, u32[]{:S(2)}, u32[]{:S(2)}) collective-permute-start(f16[7,2,32,128]{3,2,1,0:T(8,128)(2,1)S(1)} %convert_element_type.24), channel_id=1, source_target_pairs={{0,16},{8,24},{16,0},{24,8},{1,17},{9,25},{17,1},{25,9},{2,18},{10... | collective-permute-start | bytes 344072 | tf_op jit(solution)/shard_map/ppermute | solution.py:361
  6.3 0.1 collective-permute-start
  7.1 2.2 %collective-permute-done.2 = f16[7,2,32,128]{3,2,1,0:T(8,128)(2,1)S(1)} collective-permute-done((f16[7,2,32,128]{3,2,1,0:T(8,128)(2,1)S(1)}, f16[7,2,32,128]{3,2,1,0:T(8,128)(2,1)S(1)}, u32[]{:S(2)}, u32[]{:S(2)}) %collective-permute-start.2) | collective-permute-done | bytes 114720 | tf_op jit(solution)/shard_map/ppermute | solution.py:361
  9.4 2.0 %collective-permute-done.1 = f16[7,2,32,128]{3,2,1,0:T(8,128)(2,1)S(1)} collective-permute-done((f16[7,2,32,128]{3,2,1,0:T(8,128)(2,1)S(1)}, f16[7,2,32,128]{3,2,1,0:T(8,128)(2,1)S(1)}, u32[]{:S(2)}, u32[]{:S(2)}) %collective-permute-start.1) | collective-permute-done | bytes 114720 | tf_op jit(solution)/shard_map/ppermute | solution.py:361
  11.4 0.2 collective-permute-done
  11.7 0.3 shard_map.61
  12.0 0.1 collective-permute-start.3
  12.1 1.4 %collective-permute-done.3.refs_1_.refs_2_ = f32[3,4,32,128]{3,2,1,0:T(8,128)S(1)} collective-permute-done((f32[3,4,32,128]{3,2,1,0:T(8,128)S(1)}, f32[3,4,32,128]{3,2,1,0:T(8,128)S(1)}, u32[]{:S(2)}, u32[]{:S(2)}) %collective-permute-start.3) | collective-permute-done | bytes 196640 | tf_op jit(solution)/shard_map/ppermute | solution.py:385
  13.6 0.7 %collective-permute-start.4 = (f16[5,4,32,128]{3,2,1,0:T(8,128)(2,1)S(1)}, f16[5,4,32,128]{3,2,1,0:T(8,128)(2,1)S(1)}, u32[]{:S(2)}, u32[]{:S(2)}) collective-permute-start(f16[5,4,32,128]{3,2,1,0:T(8,128)(2,1)S(1)} %convert_element_type.28), channel_id=1, source_target_pairs={{1,2},{3,4},{5,6},{2,1},{4,3},{6,5},{9,10},{11,12},{13,14},{10,9},... | collective-permute-start | bytes 491528 | tf_op jit(solution)/shard_map/ppermute | solution.py:397
  14.2 0.0 collective-permute-done.4
  14.3 6.2 %collective-permute-start.5 = (f32[3,4,32,128]{3,2,1,0:T(8,128)S(1)}, f32[3,4,32,128]{3,2,1,0:T(8,128)S(1)}, u32[]{:S(2)}, u32[]{:S(2)}) collective-permute-start(f32[3,4,32,128]{3,2,1,0:T(8,128)S(1)} %shard_map.64), channel_id=1, source_target_pairs={{0,1},{1,0},{2,3},{3,2},{4,5},{5,4},{6,7},{7,6},{8,9},{9,8},{10,11... | collective-permute-start | bytes 589832 | tf_op jit(solution)/shard_map/ppermute | solution.py:413
  20.5 2.6 %collective-permute-start.6 = (f16[4,32,128]{2,1,0:T(8,128)(2,1)S(1)}, f16[4,32,128]{2,1,0:T(8,128)(2,1)S(1)}, u32[]{:S(2)}, u32[]{:S(2)}) collective-permute-start(f16[4,32,128]{2,1,0:T(8,128)(2,1)S(1)} %convert_element_type.30), channel_id=1, source_target_pairs={{0,5},{1,4},{2,7},{3,6},{4,1},{5,0},{6,3},{7,2},{8,13},{9,12},{10,... | collective-permute-start | bytes 98312 | tf_op jit(solution)/shard_map/ppermute | solution.py:401
  23.1 0.1 shard_map.60.refs_1_
  23.2 1.6 %collective-permute-done.6 = f16[4,32,128]{2,1,0:T(8,128)(2,1)S(1)} collective-permute-done((f16[4,32,128]{2,1,0:T(8,128)(2,1)S(1)}, f16[4,32,128]{2,1,0:T(8,128)(2,1)S(1)}, u32[]{:S(2)}, u32[]{:S(2)}) %collective-permute-start.6) | collective-permute-done | bytes 32800 | tf_op jit(solution)/shard_map/ppermute | solution.py:401
  24.9 1.1 %shard_map.63.refs_4_ = f32[2,4,32,128]{3,2,1,0:T(8,128)S(1)} custom-call(f32[1,128]{1,0:T(1,128)S(1)} %broadcast_in_dim.9.refs_0_, f32[3,4,32,128]{3,2,1,0:T(8,128)S(1)} %get-tuple-element.15.refs_0_.refs_1_, f32[3,4,32,128]{3,2,1,0:T(8,128)S(1)} %collective-permute-done.3.refs_1_.refs_2_, f32[4,32,128]{2,1,0:T(8,128)S(1)} %get-tuple-element.16.refs_2_.refs_3_.refs_0_, ...), custom_call_target="tpu_custom_call" | custom-call | tf_op jit(solution)/shard_map/pallas_call | solution.py:24
  26.0 0.0 collective-permute-done.5.refs_5_
  26.0 0.4 %shard_map.65 = (f32[4,2,32,128]{3,2,1,0:T(8,128)S(1)}, f32[32,1,128]{2,1,0:T(1,128)S(1)}) custom-call(f32[1,128]{1,0:T(1,128)S(1)} %broadcast_in_dim.9.refs_0_, f32[1,128]{1,0:T(1,128)S(1)} %shard_map.60.refs_1_, f32[3,1,4,2,32,128]{5,4,3,2,1,0:T(8,128)S(1)} %get-tuple-element.12.basis.refs_2_.refs_1_, ...), custom_call_target="tpu_custom_call" | custom-call | tf_op jit(solution)/shard_map/pallas_call | solution.py:24
  26.4 12.7 %all_to_all.5.refs_3_ = f32[32,1,128]{2,1,0:T(1,128)S(1)} all-to-all(f32[32,1,128]{2,1,0:T(1,128)S(1)} %get-tuple-element.19), channel_id=1, replica_groups=mesh['harm'=4,'slab'=8] {'harm','slab'}, dimensions={0} | all-to-all | bytes 32768 | tf_op jit(solution)/shard_map/all_to_all | solution.py:437
  39.1 0.8 %shard_map.66 = (f32[1,4,2,32,128]{4,3,2,1,0:T(8,128)}, f32[4]{0:T(128)}) custom-call(f32[3,128]{1,0:T(4,128)S(1)} %get-tuple-element.11.refs_0_, f32[3,1,4,2,32,128]{5,4,3,2,1,0:T(8,128)S(1)} %get-tuple-element.12.basis.refs_2_.refs_1_, f32[4,2,32,128]{3,2,1,0:T(8,128)S(1)} %get-tuple-element.18.refs_2_, f32[32,1,128]{2,1,0:T(1,128)S(1)} %all_to_all.5.refs_3_), custom_call_target="tpu_custom_call" | custom-call | tf_op jit(solution)/shard_map/pallas_call | solution.py:24
  (11 shorter events, 0.2 us)
Async XLA Ops:
  1.8 7.5 %collective-permute-start.2 = (f16[7,2,32,128]{3,2,1,0:T(8,128)(2,1)S(1)}, f16[7,2,32,128]{3,2,1,0:T(8,128)(2,1)S(1)}, u32[]{:S(2)}, u32[]{:S(2)}) collective-permute-start(f16[7,2,32,128]{3,2,1,0:T(8,128)(2,1)S(1)} %convert_element_type.24), channel_id=1, source_target_pairs={{0,24},{8,16},{16,8},{24,0},{1,25},{9,17},{17,9},{25,1},{2,26},{10... | collective-permute-start | bytes 344072 | tf_op jit(solution)/shard_map/ppermute | solution.py:361
  5.8 5.6 %collective-permute-start.1 = (f16[7,2,32,128]{3,2,1,0:T(8,128)(2,1)S(1)}, f16[7,2,32,128]{3,2,1,0:T(8,128)(2,1)S(1)}, u32[]{:S(2)}, u32[]{:S(2)}) collective-permute-start(f16[7,2,32,128]{3,2,1,0:T(8,128)(2,1)S(1)} %convert_element_type.24), channel_id=1, source_target_pairs={{0,16},{8,24},{16,0},{24,8},{1,17},{9,25},{17,1},{25,9},{2,18},{10... | collective-permute-start | bytes 344072 | tf_op jit(solution)/shard_map/ppermute | solution.py:361
  6.3 5.3 %collective-permute-start = (f16[7,2,32,128]{3,2,1,0:T(8,128)(2,1)S(1)}, f16[7,2,32,128]{3,2,1,0:T(8,128)(2,1)S(1)}, u32[]{:S(2)}, u32[]{:S(2)}) collective-permute-start(f16[7,2,32,128]{3,2,1,0:T(8,128)(2,1)S(1)} %convert_element_type.24), channel_id=1, source_target_pairs={{0,8},{8,0},{16,24},{24,16},{1,9},{9,1},{17,25},{25,17},{2,10},{10... | collective-permute-start | bytes 344072 | tf_op jit(solution)/shard_map/ppermute | solution.py:361
  12.0 1.5 %collective-permute-start.3 = (f32[3,4,32,128]{3,2,1,0:T(8,128)S(1)}, f32[3,4,32,128]{3,2,1,0:T(8,128)S(1)}, u32[]{:S(2)}, u32[]{:S(2)}) collective-permute-start(f32[3,4,32,128]{3,2,1,0:T(8,128)S(1)} %get-tuple-element.15.refs_0_.refs_1_), channel_id=1, source_target_pairs={{0,1},{1,0},{2,3},{3,2},{4,5},{5,4},{6,7},{7,6},{8,9},{9,8},{10,11... | collective-permute-start | bytes 589832 | tf_op jit(solution)/shard_map/ppermute | solution.py:385
  13.6 0.7 %collective-permute-start.4 = (f16[5,4,32,128]{3,2,1,0:T(8,128)(2,1)S(1)}, f16[5,4,32,128]{3,2,1,0:T(8,128)(2,1)S(1)}, u32[]{:S(2)}, u32[]{:S(2)}) collective-permute-start(f16[5,4,32,128]{3,2,1,0:T(8,128)(2,1)S(1)} %convert_element_type.28), channel_id=1, source_target_pairs={{1,2},{3,4},{5,6},{2,1},{4,3},{6,5},{9,10},{11,12},{13,14},{10,9},... | collective-permute-start | bytes 491528 | tf_op jit(solution)/shard_map/ppermute | solution.py:397
  14.3 11.7 %collective-permute-start.5 = (f32[3,4,32,128]{3,2,1,0:T(8,128)S(1)}, f32[3,4,32,128]{3,2,1,0:T(8,128)S(1)}, u32[]{:S(2)}, u32[]{:S(2)}) collective-permute-start(f32[3,4,32,128]{3,2,1,0:T(8,128)S(1)} %shard_map.64), channel_id=1, source_target_pairs={{0,1},{1,0},{2,3},{3,2},{4,5},{5,4},{6,7},{7,6},{8,9},{9,8},{10,11... | collective-permute-start | bytes 589832 | tf_op jit(solution)/shard_map/ppermute | solution.py:413
  20.5 4.4 %collective-permute-start.6 = (f16[4,32,128]{2,1,0:T(8,128)(2,1)S(1)}, f16[4,32,128]{2,1,0:T(8,128)(2,1)S(1)}, u32[]{:S(2)}, u32[]{:S(2)}) collective-permute-start(f16[4,32,128]{2,1,0:T(8,128)(2,1)S(1)} %convert_element_type.30), channel_id=1, source_target_pairs={{0,5},{1,4},{2,7},{3,6},{4,1},{5,0},{6,3},{7,2},{8,13},{9,12},{10,... | collective-permute-start | bytes 98312 | tf_op jit(solution)/shard_map/ppermute | solution.py:401
